TPU v7x, 32 devices: a whole 2x2x4 slice. The times are simulated.
32 devices in a mesh: grp: 2 (over x), wide: 16 (over z, y, core).
Axes of the slice: x: 2, y: 2, z: 4, core: 2. Of those that a mesh axis runs over, the one named last changes fastest.
Arguments:
- hidden_in: bfloat16 [128, 4096], P(('grp', 'wide')), parts along dimension 0, may hold values from -6 to 6
- ffn_gain: float32 [4096], replicated, may hold values from 0.1 to 1.9
- gate_weight: bfloat16 [4096, 14336], P(None, 'wide'), may hold values from -0.09375 to 0.09375
- up_weight: bfloat16 [4096, 14336], P(None, 'wide'), may hold values from -0.09375 to 0.09375
- down_weight: bfloat16 [14336, 4096], P('wide'), may hold values from -0.046875 to 0.046875
- final_gain: float32 [4096], replicated, may hold values from 0.1 to 1.9
- codes: bfloat16 [256, 128, 4096], P(('grp', 'wide')), parts along dimension 0, may hold values from -1 to 1
- scales: float32 [256, 128, 32], P(('grp', 'wide')), parts along dimension 0, may hold values from 0.5 to 5
- counts: int32 [256], P('grp'), parts along dimension 0, may hold values from 1 to 128, 10240 in all
- list_slot: int32 [256], P('grp'), parts along dimension 0, may hold values from 0 to 127, as said below
- probes: int32 [128, 8], P(('grp', 'wide')), parts along dimension 0, may hold values from 0 to 127, as said below
Outputs:
- top_scores: float32 [128, 8], P(('grp', 'wide')), parts along dimension 0
There are 2 independent parts, one for each index of `grp`. A program takes and returns all parts, laid end to end along the dimension named above; an argument that names none is the same for every part. Nothing has to cross between parts.
Inputs may be any that keep to these rules, and one draw needn't show every extreme that they name: Each query names 8 different lists. List l is held by device list_slot[l] // 8; of the 32 probes of one device's queries at most 2 name lists held by one device, and some devices are named 2 times by the queries of every device. `list_slot`: each storage row holds exactly one list. The valid rows of a list are its first counts[l] rows; some list is full.
All inputs are finite; a program needn't handle non-finite values.
Results may differ from a plain program's by a relative error of at most 0.002.
Values may be sent and summed in bfloat16 or wider, within the bound.
No kernel may reach another device: no remote copies, remote signals or barrier semaphores. Data moves between devices by JAX's collectives and lax.ppermute only.
A program may use at most 128 MiB of HBM per device.

v0:
```python
import jax
import jax.numpy as jnp
from jax import lax
from jax.sharding import PartitionSpec as P

PROBES = 8
K_TOP = 8


floor_score = -1e30


def best_values(values, count):
    return -jnp.sort(-values, axis=-1)[..., :count]


def lookup_pairs(probe_ids, list_slot, counts, lists_dev):
    flat_ids = probe_ids.reshape(-1)
    listing = jnp.arange(list_slot.shape[0], dtype=jnp.int32)
    matches = flat_ids[:, None] == listing[None, :]
    slot_of = jnp.sum(jnp.where(matches, list_slot[None, :], 0), axis=1)
    rows_of = jnp.sum(jnp.where(matches, counts[None, :], 0), axis=1)
    return (slot_of // lists_dev, slot_of % lists_dev, rows_of)


def copy_rank(owner):
    pair_total = owner.shape[-1]
    same_owner = owner[..., :, None] == owner[..., None, :]
    position = jnp.arange(pair_total, dtype=jnp.int32)
    earlier = position[:, None] > position[None, :]
    return jnp.sum(same_owner & earlier, axis=-1)


def embed(total, final_gain):
    scaled = final_gain * total
    return (scaled * lax.rsqrt(jnp.sum(scaled * scaled, axis=-1, keepdims=True) + 1e-06)).astype(
        jnp.bfloat16
    )


def score_lists(received, codes, scales):
    pair_rows, width = received.shape
    blocks = width // 128
    stored = codes.shape[0] * codes.shape[1]
    partial_sums = jnp.einsum(
        "mbk,rbk->bmr",
        received.reshape(pair_rows, blocks, 128),
        codes.reshape(stored, blocks, 128),
        preferred_element_type=jnp.float32,
    )
    return jnp.einsum(
        "bmr,rb->mr", partial_sums, scales.reshape(stored, blocks), precision=lax.Precision.HIGHEST
    )


def answer(recv_queries, recv_meta, codes, scales):
    sources, slots, width = recv_queries.shape
    lists_dev, list_rows = (codes.shape[0], codes.shape[1])
    table = score_lists(recv_queries.reshape(sources * slots, width), codes, scales)
    table = table.reshape(sources * slots, lists_dev, list_rows)
    local = recv_meta[..., 0].reshape(-1)
    valid_rows = recv_meta[..., 1].reshape(-1)
    pick_mask = local[:, None] == jnp.arange(lists_dev, dtype=jnp.int32)[None, :]
    picked = jnp.sum(jnp.where(pick_mask[:, :, None], table, 0.0), axis=1)
    alive = jnp.arange(list_rows, dtype=jnp.int32)[None, :] < valid_rows[:, None]
    masked = jnp.where(alive, picked, floor_score)
    kept = masked.reshape(sources, slots, list_rows)
    return lax.all_to_all(kept, "wide", split_axis=0, concat_axis=0, tiled=True)


def body(
    hidden_in,
    ffn_gain,
    gate_weight,
    up_weight,
    down_weight,
    final_gain,
    codes,
    scales,
    counts,
    list_slot,
    probes,
):
    q_dev, width = hidden_in.shape
    wide_count = lax.axis_size("wide")
    lists_dev = codes.shape[0]
    pair_total = q_dev * PROBES
    capacity = (pair_total + wide_count - 1) // wide_count
    own_rows = hidden_in.astype(jnp.float32)
    rows = lax.all_gather(hidden_in, "wide", axis=0, tiled=True).astype(jnp.float32)
    normed = (
        rows * lax.rsqrt(jnp.mean(rows * rows, axis=-1, keepdims=True) + 1e-05) * ffn_gain
    ).astype(jnp.bfloat16)
    gate = jnp.dot(normed, gate_weight, preferred_element_type=jnp.float32)
    upward = jnp.dot(normed, up_weight, preferred_element_type=jnp.float32)
    activated = (jax.nn.silu(gate) * upward).astype(jnp.bfloat16)
    owner, local, valid_rows = lookup_pairs(probes, list_slot, counts, lists_dev)
    target = owner * capacity + copy_rank(owner)
    mine = lax.psum_scatter(
        jnp.dot(activated, down_weight, preferred_element_type=jnp.float32),
        "wide",
        scatter_dimension=0,
        tiled=True,
    )
    embedded = embed(own_rows + mine, final_gain)
    slot_ids = jnp.arange(wide_count * capacity, dtype=jnp.int32)
    placing = slot_ids[:, None] == target[None, :]
    pair_vectors = jnp.repeat(embedded, PROBES, axis=0)
    send_queries = jnp.dot(
        placing.astype(jnp.bfloat16), pair_vectors, preferred_element_type=jnp.float32
    ).astype(jnp.bfloat16)
    send_queries = send_queries.reshape(wide_count, capacity, width)
    pair_meta = jnp.stack([local, valid_rows], axis=1)
    send_meta = jnp.sum(jnp.where(placing[:, :, None], pair_meta[None, :, :], 0), axis=1).reshape(
        wide_count, capacity, 2
    )
    returned = answer(
        lax.all_to_all(send_queries, "wide", split_axis=0, concat_axis=0, tiled=True),
        lax.all_to_all(send_meta, "wide", split_axis=0, concat_axis=0, tiled=True),
        codes,
        scales,
    )
    flat_back = returned.reshape(wide_count * capacity, returned.shape[-1])
    per_pair = jnp.take(flat_back, target, axis=0).reshape(q_dev, -1)
    return best_values(per_pair, K_TOP)


def solution(mesh):
    in_specs = (
        P(("grp", "wide"), None),
        P(),
        P(None, "wide"),
        P(None, "wide"),
        P("wide", None),
        P(),
        P(("grp", "wide"), None, None),
        P(("grp", "wide"), None, None),
        P("grp"),
        P("grp"),
        P(("grp", "wide"), None),
    )
    out_specs = P(("grp", "wide"), None)
    return jax.shard_map(body, mesh=mesh, in_specs=in_specs, out_specs=out_specs, check_vma=False)
```

profile of v0, /device:TPU:0, one launch (start us, length us, event | category | flops | bytes accessed | tf_op | source)
XLA Modules:
  0.0 191.7 jit_solution(12854098284234946222)
XLA Ops:
  6.5 24.9 %all-gather = bf16[16,4,4096]{2,1,0:T(4,128)(2,1)S(1)} all-gather(bf16[1,4,4096]{2,1,0:T(4,128)(2,1)} %bitcast.60), channel_id=1, replica_groups=mesh['grp'=2,'wide'=16] {'wide'}, dimensions={0}, use_global_device_ids=true | all-gather | bytes 557056 | tf_op jit(solution)/shard_map/all_gather | solution.py:90
  31.6 0.2 multiply_reduce_fusion.1
  31.7 4.5 %fusion.24 = f32[64,896]{1,0:T(8,128)S(1)} fusion(bf16[4096,896]{1,0:T(8,128)(2,1)} %param.13, f32[64,4096]{1,0:T(8,128)S(1)} %reshape.240, f32[4096]{0:T(1024)} %param.12, f32[64]{0:T(128)S(1)} %add_rsqrt_fusion.1), kind=kOutput, calls=%fused_computation.69 | convolution fusion | flops 470548480 | bytes 8634624 | tf_op jit(solution)/shard_map/dot_general | solution.py:94
  36.3 9.0 %fusion.5 = f32[64,4096]{1,0:T(8,128)} fusion(bf16[896,4096]{1,0:T(8,128)(2,1)} %param.15, bf16[4096,896]{1,0:T(8,128)(2,1)} %param.14, f32[64,896]{1,0:T(8,128)S(1)} %fusion.24, f32[64,4096]{1,0:T(8,128)S(1)} %reshape.240, f32[4096]{0:T(1024)S(1)} %copy-done.3, f32[64]{0:T(128)S(1)} %add_rsqrt_fusion.1), kind=kOutput, calls=%fused_computation.9 | convolution fusion | flops 940654592 | bytes 17023232 | tf_op jit(solution)/shard_map/dot_general | solution.py:100
  45.7 0.2 convert_reduce_fusion
  46.1 0.6 copy.32
  46.8 3.5 %all-to-all-start = ((s32[16,2,2]{1,2,0:T(2,128)}), s32[16,2,2]{1,2,0:T(2,128)S(1)}, u32[]{:S(2)}, u32[]{:S(2)}) async-start(s32[16,2,2]{1,2,0:T(2,128)} %copy.32), calls=%async_computation | async-start | bytes 32768 | tf_op jit(solution)/shard_map/all_to_all | solution.py:119
  50.4 0.6 dynamic-slice
  51.7 85.2 %all-reduce.3.cloned.1.call-done = f32[64,4096]{1,0:T(8,128)} async-done(((f32[64,4096]{1,0:T(8,128)}), f32[64,4096]{1,0:T(8,128)}) %all-reduce.3.cloned.1.call-update) | async-done | bytes 1048592
  137.0 1.1 multiply_reduce_fusion.2
  138.0 1.0 multiply_convert_fusion.1
  139.0 0.2 convolution_convert_fusion
  139.2 0.9 reshape.225
  140.1 3.8 %all-to-all-start.1 = ((bf16[16,2,4096]{2,1,0:T(2,128)(2,1)}), bf16[16,2,4096]{2,1,0:T(2,128)(2,1)S(1)}, u32[]{:S(2)}, u32[]{:S(2)}) async-start(bf16[16,2,4096]{2,1,0:T(2,128)(2,1)} %reshape.225), calls=%async_computation.1 | async-start | bytes 524288 | tf_op jit(solution)/shard_map/all_to_all | solution.py:118
  144.0 9.4 %copy.47 = bf16[128,8,32,128]{3,2,1,0:T(8,128)(2,1)} copy(bf16[128,8,32,128]{3,1,2,0:T(8,128)(2,1)} %bitcast.57) | data formatting | bytes 16777216
  153.6 0.3 all-to-all-done.1
  153.9 0.2 reshape_reshape.3
  154.2 12.5 %multiply_reduce_fusion = f32[1024,32]{0,1:T(8,128)S(1)} fusion(bf16[1024,32,128]{2,1,0:T(8,128)(2,1)} %bitcast.58, f32[1024,32]{0,1:T(8,128)S(1)} %copy_bitcast_fusion, bf16[32,32,128]{2,1,0:T(8,128)(2,1)S(1)} %reshape_reshape.3), kind=kOutput, calls=%fused_computation.4 | convolution fusion | flops 270499840 | bytes 8912896 | tf_op jit(solution)/shard_map/mbk,rbk->bmr/dot_general | solution.py:45
  166.9 0.7 compare_select_fusion
  167.5 5.7 %all-to-all-start.2 = ((f32[16,2,128]{2,1,0:T(2,128)}), f32[16,2,128]{2,1,0:T(2,128)S(1)}, u32[]{:S(2)}, u32[]{:S(2)}) async-start(f32[16,2,128]{2,1,0:T(2,128)} %compare_select_fusion), calls=%async_computation.2 | async-start | bytes 32768 | tf_op jit(solution)/shard_map/all_to_all | solution.py:68
  173.3 6.5 %all-to-all-done.2 = f32[16,2,128]{2,1,0:T(2,128)S(1)} async-done(((f32[16,2,128]{2,1,0:T(2,128)}), f32[16,2,128]{2,1,0:T(2,128)S(1)}, u32[]{:S(2)}, u32[]{:S(2)}) %all-to-all-start.2) | async-done | bytes 16416 | tf_op jit(solution)/shard_map/all_to_all | solution.py:68
  179.8 0.6 gather_fusion
  180.4 3.9 %sort_prefixfusion = f32[4,8]{1,0:T(4,128)S(1)} fusion(f32[4,1024]{1,0:T(4,128)S(1)} %select_negate_fusion), kind=kCustom, calls=%sort.15.sort_prefix | custom fusion | flops 49152 | bytes 16512 | tf_op jit(solution)/shard_map/jit(sort)/sort | solution.py:14
  184.3 0.6 neg.12
  (44 shorter events, 1.3 us)
Async XLA Ops:
  6.5 45.2 %copy-start = (f32[8,128,32]{1,2,0:T(8,128)S(1)}, f32[8,128,32]{1,2,0:T(8,128)}, u32[]{:S(2)}) copy-start(f32[8,128,32]{1,2,0:T(8,128)} %param.18) | copy-start | bytes 393220
  6.5 29.7 %copy-start.3 = (f32[4096]{0:T(1024)S(1)}, f32[4096]{0:T(1024)}, u32[]{:S(2)}) copy-start(f32[4096]{0:T(1024)} %param.12) | copy-start | bytes 49156
  6.5 130.4 %all-reduce.3.cloned.1.call-start = ((), (), s32[]{:S(2)}) async-start(), calls=%async_computation.3 | async-start | bytes 2097152
  36.3 9.1 %copy-start.4 = (s32[4,8]{1,0:T(4,128)S(1)}, s32[4,8]{1,0:T(4,128)}, u32[]{:S(2)}) copy-start(s32[4,8]{1,0:T(4,128)} %param.21) | copy-start | bytes 388
  36.3 9.2 %copy-start.5 = (s32[128]{0:T(128)S(1)}, s32[128]{0:T(128)}, u32[]{:S(2)}) copy-start(s32[128]{0:T(128)} %param.19) | copy-start | bytes 1540
  36.3 9.2 %copy-start.6 = (s32[128]{0:T(128)S(1)}, s32[128]{0:T(128)}, u32[]{:S(2)}) copy-start(s32[128]{0:T(128)} %param.20) | copy-start | bytes 1540
  36.3 14.1 %copy-start.7 = (u32[32]{0:T(128)S(1)}, u32[32]{0:T(128)}, u32[]{:S(2)}) copy-start(u32[32]{0:T(128)} %constant.80) | copy-start | bytes 388
  36.3 100.6 %copy-start.1 = (bf16[4,4096]{1,0:T(4,128)(2,1)S(1)}, bf16[4,4096]{1,0:T(4,128)(2,1)}, u32[]{:S(2)}) copy-start(bf16[4,4096]{1,0:T(4,128)(2,1)} %param.11) | copy-start | bytes 98308
  36.3 100.6 %copy-start.2 = (f32[4096]{0:T(1024)S(1)}, f32[4096]{0:T(1024)}, u32[]{:S(2)}) copy-start(f32[4096]{0:T(1024)} %param.16) | copy-start | bytes 49156
  46.8 93.4 %all-to-all-start = ((s32[16,2,2]{1,2,0:T(2,128)}), s32[16,2,2]{1,2,0:T(2,128)S(1)}, u32[]{:S(2)}, u32[]{:S(2)}) async-start(s32[16,2,2]{1,2,0:T(2,128)} %copy.32), calls=%async_computation | async-start | bytes 32768 | tf_op jit(solution)/shard_map/all_to_all | solution.py:119
  140.1 13.8 %all-to-all-start.1 = ((bf16[16,2,4096]{2,1,0:T(2,128)(2,1)}), bf16[16,2,4096]{2,1,0:T(2,128)(2,1)S(1)}, u32[]{:S(2)}, u32[]{:S(2)}) async-start(bf16[16,2,4096]{2,1,0:T(2,128)(2,1)} %reshape.225), calls=%async_computation.1 | async-start | bytes 524288 | tf_op jit(solution)/shard_map/all_to_all | solution.py:118
  167.5 12.2 %all-to-all-start.2 = ((f32[16,2,128]{2,1,0:T(2,128)}), f32[16,2,128]{2,1,0:T(2,128)S(1)}, u32[]{:S(2)}, u32[]{:S(2)}) async-start(f32[16,2,128]{2,1,0:T(2,128)} %compare_select_fusion), calls=%async_computation.2 | async-start | bytes 32768 | tf_op jit(solution)/shard_map/all_to_all | solution.py:68
Sparse Core Ops, SparseCore 0:
  45.5 91.3 all-reduce.2
where the time goes:
time: 192 us
  waiting for transfers between devices  92 us (48%)
  matrix products  26.3 us (14%)
  blocking collectives  24.9 us (13%)
  between operations  14.3 us (7%)
  local copies, waits for them, and re-layouts  13 us (7%)
  starting transfers between devices  13 us (7%)
  other arithmetic  8.15 us (4%)
    unnamed x2, waiting for transfers between devices  85.2 us
    all_gather x1, blocking collectives, body(): lax.all_gather(hidden_in, 'wide', axis=0, tiled=True).astype(jnp.float32)  24.9 us
    dot_general x1, matrix products, score_lists(): jnp.einsum('mbk,rbk->bmr', received.reshape(pair_rows, blocks, 128), code...  12.5 us
    unnamed x20, local copies, waits for them, and re-layouts  10.2 us
    dot_general x1, matrix products, body(): jnp.dot(activated, down_weight, preferred_element_type=jnp.float32)  9.03 us
    all_to_all x1, waiting for transfers between devices, answer(): return lax.all_to_all(kept, 'wide', split_axis=0, concat_axis=0, tiled=True)  6.49 us
    all_to_all x1, starting transfers between devices, answer(): return lax.all_to_all(kept, 'wide', split_axis=0, concat_axis=0, tiled=True)  5.72 us
    dot_general x1, matrix products, body(): gate = jnp.dot(normed, gate_weight, preferred_element_type=jnp.float32)  4.51 us
  transfers between devices with their start and end apart: 4, of which 3 were waited for; matrix products, arithmetic and copies ran while one was open for 8% of the time, Pallas kernels for 0%

commit v1 on v0

v1 whole, which is shorter than its diff:
```python
import functools

import jax
import jax.numpy as jnp
from jax import lax
from jax.experimental import pallas as pl
from jax.experimental.pallas import tpu as pltpu
from jax.sharding import PartitionSpec as P

PROBES = 8
K_TOP = 8
BLOCK = 128
LANES = 128

floor_score = -1e30

VMEM = pltpu.VMEM


def call(kernel, out_shape, args, vmem, cost=None, scratch=()):
    many = isinstance(out_shape, (list, tuple))
    return pl.pallas_call(
        kernel,
        out_shape=out_shape,
        in_specs=[pl.BlockSpec(memory_space=VMEM)] * len(args),
        out_specs=[pl.BlockSpec(memory_space=VMEM)] * len(out_shape)
        if many
        else pl.BlockSpec(memory_space=VMEM),
        scratch_shapes=list(scratch),
        compiler_params=pltpu.CompilerParams(vmem_limit_bytes=vmem),
        cost_estimate=cost,
    )(*args)


def shaped(shape, dtype):
    return jax.ShapeDtypeStruct(shape, dtype)


def norm_kernel(hidden_ref, gain_ref, out_ref):
    rows = hidden_ref[...].astype(jnp.float32)
    scale = lax.rsqrt(jnp.mean(rows * rows, axis=-1, keepdims=True) + 1e-05)
    normed = (rows * scale * gain_ref[...]).astype(jnp.bfloat16)
    for k in range(out_ref.shape[0]):
        out_ref[k] = normed


def route_kernel(lists_dev, capacity, probes_ref, slot_ref, count_ref, out_ref):
    q_dev, probes = probes_ref.shape
    lists = slot_ref.shape[1]
    pairs = q_dev * probes
    slots = out_ref.shape[0]
    ids = jnp.concatenate(
        [jnp.broadcast_to(probes_ref[q : q + 1, :], (probes, probes)) for q in range(q_dev)], axis=0
    )
    sub = lax.broadcasted_iota(jnp.int32, (pairs, probes), 0)
    lane = lax.broadcasted_iota(jnp.int32, (pairs, probes), 1)
    ids = jnp.sum(jnp.where(sub % probes == lane, ids, 0), axis=1, keepdims=True)
    hit = lax.broadcasted_iota(jnp.int32, (pairs, lists), 1) == ids
    slot = jnp.sum(jnp.where(hit, slot_ref[...], 0), axis=1, keepdims=True)
    valid = jnp.sum(jnp.where(hit, count_ref[...], 0), axis=1, keepdims=True)
    owner = slot // lists_dev
    local = slot % lists_dev
    p_sub = lax.broadcasted_iota(jnp.int32, (pairs, pairs), 0)
    p_lane = lax.broadcasted_iota(jnp.int32, (pairs, pairs), 1)
    diagonal = p_sub == p_lane

    def as_row(column):
        return jnp.sum(jnp.where(diagonal, column, 0), axis=0, keepdims=True)

    owner_row = as_row(owner)
    rank_row = jnp.sum(
        jnp.where((owner == owner_row) & (p_sub < p_lane), 1, 0), axis=0, keepdims=True
    )
    target_row = owner_row * capacity + rank_row
    here = lax.broadcasted_iota(jnp.int32, (slots, pairs), 0) == target_row
    pair_row = lax.broadcasted_iota(jnp.int32, (slots, pairs), 1)

    def of_slot(row):
        return jnp.sum(jnp.where(here, row, 0), axis=1, keepdims=True)

    query = of_slot(pair_row // probes + 1) - 1
    place = lax.broadcasted_iota(jnp.int32, (slots, LANES), 1)
    out = jnp.where(place == 0, query, 0)
    out = jnp.where(place == 1, of_slot(as_row(local)), out)
    out_ref[...] = jnp.where(place == 2, of_slot(as_row(valid)), out)


def ffn_kernel(
    k_chunk, n_chunk, same_ref, other_ref, gate_ref, up_ref, down_ref, own_ref, send_ref,
    rows_ref, gate_acc, up_acc, act_ref,
):
    chips, q_dev, width = same_ref.shape
    half = chips * q_dev
    rows_ref[:half, :] = same_ref[...].reshape(half, width)
    rows_ref[half:, :] = other_ref[...].reshape(half, width)
    gate_acc[...] = jnp.zeros_like(gate_acc)
    up_acc[...] = jnp.zeros_like(up_acc)

    @pl.loop(0, width // k_chunk)
    def _(step):
        span = pl.ds(pl.multiple_of(step * k_chunk, k_chunk), k_chunk)
        x = rows_ref[:, span]
        gate_acc[...] += jnp.dot(x, gate_ref[span, :], preferred_element_type=jnp.float32)
        up_acc[...] += jnp.dot(x, up_ref[span, :], preferred_element_type=jnp.float32)

    gate = gate_acc[...]
    act_ref[...] = (gate / (1.0 + jnp.exp(-gate)) * up_acc[...]).astype(jnp.bfloat16)

    @pl.loop(0, width // n_chunk)
    def _(step):
        span = pl.ds(pl.multiple_of(step * n_chunk, n_chunk), n_chunk)
        out = jnp.dot(act_ref[...], down_ref[:, span], preferred_element_type=jnp.float32)
        own_ref[:, span] = out[:half]
        send_ref[:, span] = out[half:].astype(jnp.bfloat16)


def add_kernel(own_ref, came_ref, out_ref):
    total = own_ref[...] + came_ref[...].astype(jnp.float32)
    out_ref[...] = total.astype(jnp.bfloat16).reshape(out_ref.shape)


def embed_kernel(parts_ref, hidden_ref, gain_ref, route_ref, out_ref):
    chips, q_dev, width = parts_ref.shape
    total = parts_ref[0].astype(jnp.float32)
    for k in range(1, chips):
        total += parts_ref[k].astype(jnp.float32)
    scaled = gain_ref[...] * (hidden_ref[...].astype(jnp.float32) + total)
    embedded = scaled * lax.rsqrt(jnp.sum(scaled * scaled, axis=-1, keepdims=True) + 1e-06)
    query = route_ref[:, 0:1]
    sent = jnp.zeros((query.shape[0], width), jnp.float32)
    for q in range(q_dev):
        sent = jnp.where(query == q, embedded[q : q + 1, :], sent)
    out_ref[:, :, :width] = sent.astype(jnp.bfloat16).reshape(out_ref.shape[:2] + (width,))
    lane = lax.broadcasted_iota(jnp.int32, (query.shape[0], LANES), 1)
    local = jnp.where(lane == 0, route_ref[:, 1:2], 0).astype(jnp.float32)
    out_ref[:, :, width:] = local.astype(jnp.bfloat16).reshape(out_ref.shape[:2] + (LANES,))


def score_kernel(came_ref, codes_ref, scales_ref, out_ref, rows_ref):
    sources, slots, _ = came_ref.shape
    lists, list_rows, width = codes_ref.shape
    pairs = sources * slots
    rows_ref[...] = came_ref[...].reshape(rows_ref.shape)
    local = rows_ref[:, width : width + 1].astype(jnp.float32).astype(jnp.int32)

    def one_list(index, picked):
        scale = scales_ref[index]
        total = jnp.zeros((pairs, list_rows), jnp.float32)
        for block in range(width // BLOCK):
            span = slice(block * BLOCK, (block + 1) * BLOCK)
            part = lax.dot_general(
                rows_ref[:, span],
                codes_ref[index, :, span],
                (((1,), (1,)), ((), ())),
                preferred_element_type=jnp.float32,
            )
            total += part * scale[block : block + 1, :]
        return jnp.where(local == index, total, picked)

    picked = lax.fori_loop(0, lists, one_list, jnp.zeros((pairs, list_rows), jnp.float32))
    out_ref[...] = picked.reshape(out_ref.shape)


def best_kernel(back_ref, route_ref, out_ref):
    q_dev, count = out_ref.shape
    sources, slots, list_rows = back_ref.shape
    pairs = sources * slots
    scores = back_ref[...].reshape(pairs, list_rows)
    query = route_ref[:, 0:1]
    row = lax.broadcasted_iota(jnp.int32, (pairs, list_rows), 1)
    place = lax.broadcasted_iota(jnp.int32, (pairs, list_rows), 0) * list_rows + row
    alive = row < route_ref[:, 2:3]
    column = lax.broadcasted_iota(jnp.int32, (1, count), 1)
    for q in range(q_dev):
        left = jnp.where(alive & (query == q), scores, floor_score)
        best = jnp.zeros((1, count), jnp.float32)
        for rank in range(count):
            top = jnp.max(left, axis=(0, 1), keepdims=True)
            best = jnp.where(column == rank, top, best)
            if rank + 1 < count:
                first = jnp.min(
                    jnp.where(left == top, place, pairs * list_rows), axis=(0, 1), keepdims=True
                )
                left = jnp.where(place == first, floor_score * 2, left)
        out_ref[q : q + 1, :] = best


def body(
    hidden_in,
    ffn_gain,
    gate_weight,
    up_weight,
    down_weight,
    final_gain,
    codes,
    scales,
    counts,
    list_slot,
    probes,
):
    q_dev, width = hidden_in.shape
    hidden_units = gate_weight.shape[1]
    n = lax.axis_size("wide")
    chips = n // 2
    half = chips * q_dev
    rows = 2 * half
    lists_dev, list_rows, _ = codes.shape
    capacity = (q_dev * PROBES + n - 1) // n
    groups = [[core + 2 * k for k in range(chips)] for core in range(2)]
    swap = [(i, i ^ 1) for i in range(n)]
    mib = 1 << 20
    f32, bf16 = jnp.float32, jnp.bfloat16

    def exchange(x, axis_index_groups=None):
        return lax.all_to_all(
            x, "wide", 0, 0, axis_index_groups=axis_index_groups, tiled=True
        )

    gate_near = pltpu.with_memory_space_constraint(gate_weight, VMEM)
    up_near = pltpu.with_memory_space_constraint(up_weight, VMEM)
    down_near = pltpu.with_memory_space_constraint(down_weight, VMEM)
    codes_near = pltpu.with_memory_space_constraint(codes, VMEM)

    normed = call(
        norm_kernel, shaped((chips, q_dev, width), bf16), (hidden_in, ffn_gain[None]), 8 * mib
    )
    route = call(
        functools.partial(route_kernel, lists_dev, capacity),
        shaped((n * capacity, LANES), jnp.int32),
        (probes, list_slot[None], counts[None]),
        8 * mib,
    )
    same = exchange(normed, groups)
    other = lax.ppermute(same, "wide", swap)
    own, sent = call(
        functools.partial(ffn_kernel, 512, 512),
        [shaped((half, width), f32), shaped((half, width), bf16)],
        (same, other, gate_near, up_near, down_near),
        20 * mib,
        scratch=[
            VMEM((rows, width), bf16),
            VMEM((rows, hidden_units), f32),
            VMEM((rows, hidden_units), f32),
            VMEM((rows, hidden_units), bf16),
        ],
    )
    came = lax.ppermute(sent, "wide", swap)
    pairs_sum = call(add_kernel, shaped((chips, q_dev, width), bf16), (own, came), 16 * mib)
    parts = exchange(pairs_sum, groups)
    queries = call(
        embed_kernel,
        shaped((n, capacity, width + LANES), bf16),
        (parts, hidden_in, final_gain[None], route),
        16 * mib,
    )
    recv = exchange(queries)
    scores = call(
        score_kernel,
        shaped((n, capacity, list_rows), f32),
        (recv, codes_near, jnp.swapaxes(scales, 1, 2)),
        20 * mib,
        scratch=[VMEM((n * capacity, width + LANES), bf16)],
    )
    back = exchange(scores)
    return call(best_kernel, shaped((q_dev, K_TOP), f32), (back, route), 8 * mib)


def solution(mesh):
    in_specs = (
        P(("grp", "wide"), None),
        P(),
        P(None, "wide"),
        P(None, "wide"),
        P("wide", None),
        P(),
        P(("grp", "wide"), None, None),
        P(("grp", "wide"), None, None),
        P("grp"),
        P("grp"),
        P(("grp", "wide"), None),
    )
    out_specs = P(("grp", "wide"), None)
    return jax.shard_map(body, mesh=mesh, in_specs=in_specs, out_specs=out_specs, check_vma=False)
```

time: 192 us -> 92 us (0.48)
  waiting for transfers between devices: 92 us -> 11.9 us
  matrix products: 26.3 us -> 0 us
  Pallas kernels: 0 us -> 22.5 us
  between operations: 14.3 us -> 0.12 us
  blocking collectives: 24.9 us -> 39 us
  starting transfers between devices: 13 us -> 3.79 us
  other arithmetic: 8.15 us -> 0 us
    unnamed x2 -> x0, waiting for transfers between devices: 85.2 us -> none
    all_to_all x0 -> x3, blocking collectives: none -> 39 us  [exchange(): lax.all_to_all(x, 'wide', 0, 0, axis_index_groups=axis_index_groups, tile...]
    dot_general x4 -> x0, matrix products: 26.3 us -> none  [the longest x1 12.5 us: score_lists(): jnp.einsum('mbk,rbk->bmr', received.reshape(pair_rows, blocks, 128), code...]
    all_gather x1 -> x0, blocking collectives: 24.9 us -> none  [body(): lax.all_gather(hidden_in, 'wide', axis=0, tiled=True).astype(jnp.float32)]
    pallas_call x0 -> x7, Pallas kernels: none -> 22.5 us  [call(): pl.pallas_call(kernel, out_shape=out_shape, in_specs=[pl.BlockSpec(memory...]
    all_to_all x3 -> x1, starting transfers between devices: 13 us -> 3.59 us  [exchange(): lax.all_to_all(x, 'wide', 0, 0, axis_index_groups=axis_index_groups, tile...]
    unnamed x20 -> x24, local copies, waits for them, and re-layouts: 10.2 us -> 14.1 us
    sort x1 -> x0, other arithmetic: 3.89 us -> none  [best_values(): return -jnp.sort(-values, axis=-1)[..., :count]]
  transfers between devices with their start and end apart: 4 -> 3, of which waited for: 3 -> 3; matrix products, arithmetic and copies ran while one was open for 8% -> 0% of each run, Pallas kernels for 0% -> 0%
where the time goes in v1:
time: 92 us; the launch traced here: 91.4 us
  blocking collectives  39 us (42%)
  Pallas kernels  22.5 us (24%)
  local copies, waits for them, and re-layouts  14.1 us (15%)
  waiting for transfers between devices  11.9 us (13%)
  starting transfers between devices  3.79 us (4%)
    all_to_all x3, blocking collectives, exchange(): lax.all_to_all(x, 'wide', 0, 0, axis_index_groups=axis_index_groups, tile...  39 us
    pallas_call x7, Pallas kernels, call(): pl.pallas_call(kernel, out_shape=out_shape, in_specs=[pl.BlockSpec(memory...  22.5 us
    unnamed x24, local copies, waits for them, and re-layouts  14.1 us
    all_to_all x1, waiting for transfers between devices, exchange(): lax.all_to_all(x, 'wide', 0, 0, axis_index_groups=axis_index_groups, tile...  8.93 us
    all_to_all x1, starting transfers between devices, exchange(): lax.all_to_all(x, 'wide', 0, 0, axis_index_groups=axis_index_groups, tile...  3.59 us
  transfers between devices with their start and end apart: 3, of which 3 were waited for; matrix products, arithmetic and copies ran while one was open for 0% of the time, Pallas kernels for 0%

profile of v1, /device:TPU:0, one launch (start us, length us, event | category | flops | bytes accessed | tf_op | source)
XLA Modules:
  0.0 91.4 jit_solution(15283210208234967371)
XLA Ops:
  0.0 0.8 copy-done.5
  0.8 0.7 copy-done.7
  1.5 0.1 shard_map.109
  1.6 0.0 copy-start.10
  1.7 0.0 copy-start.11
  1.7 0.0 copy-start.4
  1.7 16.2 %all_to_all.20.same_ref = bf16[8,4,4096]{2,1,0:T(4,128)(2,1)S(1)} all-to-all(bf16[8,4,4096]{2,1,0:T(4,128)(2,1)S(1)} %shard_map.109), channel_id=1, replica_groups={{0,2,4,6,8,10,12,14},{1,3,5,7,9,11,13,15},{16,18,20,22,24,26,28,30},{17..., dimensions={0} | all-to-all | bytes 524288 | tf_op jit(solution)/shard_map/all_to_all | solution.py:215
  17.9 1.5 %collective-permute-done.other_ref = bf16[8,4,4096]{2,1,0:T(4,128)(2,1)S(1)} collective-permute-done((bf16[8,4,4096]{2,1,0:T(4,128)(2,1)S(1)}, bf16[8,4,4096]{2,1,0:T(4,128)(2,1)S(1)}, u32[]{:S(2)}, u32[]{:S(2)}) %collective-permute-start) | collective-permute-done | bytes 262176 | tf_op jit(solution)/shard_map/ppermute | solution.py:234
  19.4 3.1 %copy-done.1 = bf16[4096,896]{1,0:T(8,128)(2,1)S(1)} copy-done((bf16[4096,896]{1,0:T(8,128)(2,1)S(1)}, bf16[4096,896]{1,0:T(8,128)(2,1)}, u32[]{:S(2)}) %copy-start.1) | copy-done | bytes 7340056
  22.5 3.1 %copy-done.2 = bf16[4096,896]{1,0:T(8,128)(2,1)S(1)} copy-done((bf16[4096,896]{1,0:T(8,128)(2,1)S(1)}, bf16[4096,896]{1,0:T(8,128)(2,1)}, u32[]{:S(2)}) %copy-start.2) | copy-done | bytes 7340056
  25.6 3.1 %copy-done.3 = bf16[896,4096]{1,0:T(8,128)(2,1)S(1)} copy-done((bf16[896,4096]{1,0:T(8,128)(2,1)S(1)}, bf16[896,4096]{1,0:T(8,128)(2,1)}, u32[]{:S(2)}) %copy-start.3) | copy-done | bytes 7340056
  28.6 6.0 %shard_map.110 = (f32[32,4096]{1,0:T(8,128)S(1)}, bf16[32,4096]{1,0:T(8,128)(2,1)S(1)}) custom-call(bf16[8,4,4096]{2,1,0:T(4,128)(2,1)S(1)} %all_to_all.20.same_ref, bf16[8,4,4096]{2,1,0:T(4,128)(2,1)S(1)} %collective-permute-done.other_ref, bf16[4096,896]{1,0:T(8,128)(2,1)S(1)} %copy-done.1, bf16[4096,896]{1,0:T(8,128)(2,1)S(1)} %copy-done.2, ...), custom_call_target="tpu_custom_call" | custom-call | tf_op jit(solution)/shard_map/pallas_call | solution.py:22
  34.6 0.2 collective-permute-start.1
  34.8 1.4 %collective-permute-done.1.came_ref = bf16[32,4096]{1,0:T(8,128)(2,1)S(1)} collective-permute-done((bf16[32,4096]{1,0:T(8,128)(2,1)S(1)}, bf16[32,4096]{1,0:T(8,128)(2,1)S(1)}, u32[]{:S(2)}, u32[]{:S(2)}) %collective-permute-start.1) | collective-permute-done | bytes 262176 | tf_op jit(solution)/shard_map/ppermute | solution.py:247
  36.2 0.8 shard_map.111
  37.0 3.6 %all-to-all-start.1 = ((bf16[8,4,4096]{2,1,0:T(4,128)(2,1)}), bf16[8,4,4096]{2,1,0:T(4,128)(2,1)S(1)}, u32[]{:S(2)}, u32[]{:S(2)}) async-start(bf16[8,4,4096]{2,1,0:T(4,128)(2,1)} %shard_map.111), calls=%async_computation.1 | async-start | bytes 524288 | tf_op jit(solution)/shard_map/all_to_all | solution.py:215
  40.6 0.3 shard_map.112.route_ref
  40.9 8.9 %all-to-all-done.1.parts_ref = bf16[8,4,4096]{2,1,0:T(4,128)(2,1)S(1)} async-done(((bf16[8,4,4096]{2,1,0:T(4,128)(2,1)}), bf16[8,4,4096]{2,1,0:T(4,128)(2,1)S(1)}, u32[]{:S(2)}, u32[]{:S(2)}) %all-to-all-start.1) | async-done | bytes 262176 | tf_op jit(solution)/shard_map/all_to_all | solution.py:215
  49.8 0.3 shard_map.113
  50.2 13.6 %all_to_all.21.came_ref = bf16[16,2,4224]{2,1,0:T(2,128)(2,1)S(1)} all-to-all(bf16[16,2,4224]{2,1,0:T(2,128)(2,1)S(1)} %shard_map.113), channel_id=1, replica_groups=mesh['grp'=2,'wide'=16] {'wide'}, dimensions={0} | all-to-all | bytes 540672 | tf_op jit(solution)/shard_map/all_to_all | solution.py:215
  63.8 3.4 %copy-done = bf16[8,128,4096]{2,1,0:T(8,128)(2,1)S(1)} copy-done((bf16[8,128,4096]{2,1,0:T(8,128)(2,1)S(1)}, bf16[8,128,4096]{2,1,0:T(8,128)(2,1)}, u32[]{:S(2)}) %copy-start) | copy-done | bytes 8388632
  67.2 5.4 %shard_map.114 = f32[16,2,128]{2,1,0:T(2,128)S(1)} custom-call(bf16[16,2,4224]{2,1,0:T(2,128)(2,1)S(1)} %all_to_all.21.came_ref, bf16[8,128,4096]{2,1,0:T(8,128)(2,1)S(1)} %copy-done, f32[8,32,128]{2,1,0:T(8,128)S(1)} %bitcast.5), custom_call_target="tpu_custom_call" | custom-call | tf_op jit(solution)/shard_map/pallas_call | solution.py:22
  72.6 9.2 %all_to_all.22.back_ref = f32[16,2,128]{2,1,0:T(2,128)S(1)} all-to-all(f32[16,2,128]{2,1,0:T(2,128)S(1)} %shard_map.114), channel_id=1, replica_groups=mesh['grp'=2,'wide'=16] {'wide'}, dimensions={0} | all-to-all | bytes 32768 | tf_op jit(solution)/shard_map/all_to_all | solution.py:215
  81.8 9.6 %shard_map.115 = f32[4,8]{1,0:T(4,128)} custom-call(f32[16,2,128]{2,1,0:T(2,128)S(1)} %all_to_all.22.back_ref, s32[32,128]{1,0:T(8,128)S(1)} %shard_map.112.route_ref), custom_call_target="tpu_custom_call" | custom-call | tf_op jit(solution)/shard_map/pallas_call | solution.py:22
  (16 shorter events, 0.0 us)
Async XLA Ops:
  0.0 0.8 copy-start.5
  0.8 0.7 copy-start.7
  1.6 38.9 %copy-start.9 = (s32[4,8]{1,0:T(4,128)S(1)}, s32[4,8]{1,0:T(4,128)}, u32[]{:S(2)}) copy-start(s32[4,8]{1,0:T(4,128)} %probes_ref.1) | copy-start | bytes 388
  1.6 38.9 %copy-start.10 = (s32[128]{0:T(128)S(1)}, s32[128]{0:T(128)}, u32[]{:S(2)}) copy-start(s32[128]{0:T(128)} %param.20) | copy-start | bytes 1540
  1.7 38.9 %copy-start.11 = (s32[128]{0:T(128)S(1)}, s32[128]{0:T(128)}, u32[]{:S(2)}) copy-start(s32[128]{0:T(128)} %param.19) | copy-start | bytes 1540
  1.7 48.2 %copy-start.6 = (bf16[4,4096]{1,0:T(4,128)(2,1)S(1)}, bf16[4,4096]{1,0:T(4,128)(2,1)}, u32[]{:S(2)}) copy-start(bf16[4,4096]{1,0:T(4,128)(2,1)} %hidden_ref.3) | copy-start | bytes 98308
  1.7 48.2 %copy-start.8 = (f32[4096]{0:T(1024)S(1)}, f32[4096]{0:T(1024)}, u32[]{:S(2)}) copy-start(f32[4096]{0:T(1024)} %param.16) | copy-start | bytes 49156
  1.7 62.1 %copy-start.4 = (f32[8,128,32]{1,2,0:T(8,128)S(1)}, f32[8,128,32]{1,2,0:T(8,128)}, u32[]{:S(2)}) copy-start(f32[8,128,32]{1,2,0:T(8,128)} %param.18) | copy-start | bytes 393220
  17.9 1.5 %collective-permute-start = (bf16[8,4,4096]{2,1,0:T(4,128)(2,1)S(1)}, bf16[8,4,4096]{2,1,0:T(4,128)(2,1)S(1)}, u32[]{:S(2)}, u32[]{:S(2)}) collective-permute-start(bf16[8,4,4096]{2,1,0:T(4,128)(2,1)S(1)} %all_to_all.20.same_ref), channel_id=1, source_target_pairs={{0,1},{1,0},{2,3},{3,2},{4,5},{5,4},{6,7},{7,6},{8,9},{9,8},{10,11... | collective-permute-start | bytes 786440 | tf_op jit(solution)/shard_map/ppermute | solution.py:234
  19.4 3.1 %copy-start.1 = (bf16[4096,896]{1,0:T(8,128)(2,1)S(1)}, bf16[4096,896]{1,0:T(8,128)(2,1)}, u32[]{:S(2)}) copy-start(bf16[4096,896]{1,0:T(8,128)(2,1)} %gate_ref.1) | copy-start | bytes 22020100
  22.5 3.1 %copy-start.2 = (bf16[4096,896]{1,0:T(8,128)(2,1)S(1)}, bf16[4096,896]{1,0:T(8,128)(2,1)}, u32[]{:S(2)}) copy-start(bf16[4096,896]{1,0:T(8,128)(2,1)} %up_ref.1) | copy-start | bytes 22020100
  25.6 3.1 %copy-start.3 = (bf16[896,4096]{1,0:T(8,128)(2,1)S(1)}, bf16[896,4096]{1,0:T(8,128)(2,1)}, u32[]{:S(2)}) copy-start(bf16[896,4096]{1,0:T(8,128)(2,1)} %down_ref.1) | copy-start | bytes 22020100
  34.6 1.6 %collective-permute-start.1 = (bf16[32,4096]{1,0:T(8,128)(2,1)S(1)}, bf16[32,4096]{1,0:T(8,128)(2,1)S(1)}, u32[]{:S(2)}, u32[]{:S(2)}) collective-permute-start(bf16[32,4096]{1,0:T(8,128)(2,1)S(1)} %get-tuple-element.8), channel_id=1, source_target_pairs={{0,1},{1,0},{2,3},{3,2},{4,5},{5,4},{6,7},{7,6},{8,9},{9,8},{10,11... | collective-permute-start | bytes 786440 | tf_op jit(solution)/shard_map/ppermute | solution.py:247
  37.0 12.9 %all-to-all-start.1 = ((bf16[8,4,4096]{2,1,0:T(4,128)(2,1)}), bf16[8,4,4096]{2,1,0:T(4,128)(2,1)S(1)}, u32[]{:S(2)}, u32[]{:S(2)}) async-start(bf16[8,4,4096]{2,1,0:T(4,128)(2,1)} %shard_map.111), calls=%async_computation.1 | async-start | bytes 524288 | tf_op jit(solution)/shard_map/all_to_all | solution.py:215
  63.8 3.4 %copy-start = (bf16[8,128,4096]{2,1,0:T(8,128)(2,1)S(1)}, bf16[8,128,4096]{2,1,0:T(8,128)(2,1)}, u32[]{:S(2)}) copy-start(bf16[8,128,4096]{2,1,0:T(8,128)(2,1)} %codes_ref.1) | copy-start | bytes 25165828

commit v2 on v1

--- a/solution.py
+++ b/solution.py
@@ -32,6 +32,11 @@
     )(*args)
 
 
+def ahead(*arrays):
+    total = sum(a.size * a.dtype.itemsize for a in arrays)
+    return pl.CostEstimate(flops=1000 * total, bytes_accessed=1 << 20, transcendentals=0)
+
+
 def shaped(shape, dtype):
     return jax.ShapeDtypeStruct(shape, dtype)
 
@@ -44,7 +49,7 @@
         out_ref[k] = normed
 
 
-def route_kernel(lists_dev, capacity, probes_ref, slot_ref, count_ref, out_ref):
+def route_kernel(lists_dev, capacity, probes_ref, slot_ref, count_ref, after_ref, out_ref):
     q_dev, probes = probes_ref.shape
     lists = slot_ref.shape[1]
     pairs = q_dev * probes
@@ -86,7 +91,7 @@
 
 
 def ffn_kernel(
-    k_chunk, n_chunk, same_ref, other_ref, gate_ref, up_ref, down_ref, own_ref, send_ref,
+    k_chunk, n_chunk, same_ref, other_ref, gate_ref, up_ref, down_ref, after_ref, own_ref, send_ref,
     rows_ref, gate_acc, up_acc, act_ref,
 ):
     chips, q_dev, width = same_ref.shape
@@ -140,24 +145,33 @@
     sources, slots, _ = came_ref.shape
     lists, list_rows, width = codes_ref.shape
     pairs = sources * slots
-    rows_ref[...] = came_ref[...].reshape(rows_ref.shape)
-    local = rows_ref[:, width : width + 1].astype(jnp.float32).astype(jnp.int32)
-
-    def one_list(index, picked):
-        scale = scales_ref[index]
-        total = jnp.zeros((pairs, list_rows), jnp.float32)
-        for block in range(width // BLOCK):
-            span = slice(block * BLOCK, (block + 1) * BLOCK)
+    came = came_ref[...].reshape(pairs, width + LANES)
+    nothing = jnp.zeros((pairs, BLOCK), jnp.bfloat16)
+    for block in range(width // BLOCK):
+        span = slice(block * BLOCK, (block + 1) * BLOCK)
+        kept = block % 2
+        rows_ref[kept * pairs : (kept + 1) * pairs, span] = came[:, span]
+        rows_ref[(1 - kept) * pairs : (2 - kept) * pairs, span] = nothing
+    local = came[:, width : width + 1].astype(jnp.float32).astype(jnp.int32)
+
+    def two_lists(index, picked):
+        first = index * 2
+        scale = jnp.concatenate([scales_ref[first], scales_ref[first + 1]], axis=1)
+        total = jnp.zeros((pairs, 2 * list_rows), jnp.float32)
+        for step in range(width // (2 * BLOCK)):
+            span = slice(step * 2 * BLOCK, (step + 1) * 2 * BLOCK)
             part = lax.dot_general(
                 rows_ref[:, span],
-                codes_ref[index, :, span],
+                codes_ref[pl.ds(first, 2), :, span].reshape(2 * list_rows, 2 * BLOCK),
                 (((1,), (1,)), ((), ())),
                 preferred_element_type=jnp.float32,
             )
-            total += part * scale[block : block + 1, :]
-        return jnp.where(local == index, total, picked)
-
-    picked = lax.fori_loop(0, lists, one_list, jnp.zeros((pairs, list_rows), jnp.float32))
+            total += part[:pairs] * scale[2 * step : 2 * step + 1, :]
+            total += part[pairs:] * scale[2 * step + 1 : 2 * step + 2, :]
+        picked = jnp.where(local == first, total[:, :list_rows], picked)
+        return jnp.where(local == first + 1, total[:, list_rows:], picked)
+
+    picked = lax.fori_loop(0, lists // 2, two_lists, jnp.zeros((pairs, list_rows), jnp.float32))
     out_ref[...] = picked.reshape(out_ref.shape)
 
 
@@ -167,22 +181,23 @@
     pairs = sources * slots
     scores = back_ref[...].reshape(pairs, list_rows)
     query = route_ref[:, 0:1]
-    row = lax.broadcasted_iota(jnp.int32, (pairs, list_rows), 1)
-    place = lax.broadcasted_iota(jnp.int32, (pairs, list_rows), 0) * list_rows + row
-    alive = row < route_ref[:, 2:3]
-    column = lax.broadcasted_iota(jnp.int32, (1, count), 1)
-    for q in range(q_dev):
-        left = jnp.where(alive & (query == q), scores, floor_score)
-        best = jnp.zeros((1, count), jnp.float32)
-        for rank in range(count):
-            top = jnp.max(left, axis=(0, 1), keepdims=True)
-            best = jnp.where(column == rank, top, best)
-            if rank + 1 < count:
-                first = jnp.min(
-                    jnp.where(left == top, place, pairs * list_rows), axis=(0, 1), keepdims=True
-                )
-                left = jnp.where(place == first, floor_score * 2, left)
-        out_ref[q : q + 1, :] = best
+    alive = lax.broadcasted_iota(jnp.int32, (pairs, list_rows), 1) < route_ref[:, 2:3]
+    left = jnp.concatenate(
+        [jnp.where(alive & (query == q), scores, floor_score)[None] for q in range(q_dev)], axis=0
+    )
+    column = lax.broadcasted_iota(jnp.int32, (q_dev, count), 1)
+    best = jnp.zeros((q_dev, count), jnp.float32)
+    filled = jnp.zeros((q_dev, 1), jnp.float32)
+    for rank in range(count):
+        top = jnp.max(jnp.max(left, axis=1), axis=-1, keepdims=True)
+        best = jnp.where(column >= filled.astype(jnp.int32), top, best)
+        if rank + 1 < count:
+            same = left == top[:, :, None]
+            filled += jnp.sum(
+                jnp.sum(jnp.where(same, 1.0, 0.0), axis=1), axis=-1, keepdims=True
+            )
+            left = jnp.where(same, floor_score * 2, left)
+    out_ref[...] = best
 
 
 def body(
@@ -222,20 +237,21 @@
     codes_near = pltpu.with_memory_space_constraint(codes, VMEM)
 
     normed = call(
-        norm_kernel, shaped((chips, q_dev, width), bf16), (hidden_in, ffn_gain[None]), 8 * mib
-    )
+        norm_kernel, shaped((chips, q_dev, width), bf16), (hidden_in, ffn_gain[None]), 8 * mib,
+        cost=ahead(gate_weight, up_weight, down_weight),
+    )
+    same = exchange(normed, groups)
+    other = lax.ppermute(same, "wide", swap)
     route = call(
         functools.partial(route_kernel, lists_dev, capacity),
         shaped((n * capacity, LANES), jnp.int32),
-        (probes, list_slot[None], counts[None]),
+        (probes, list_slot[None], counts[None], same),
         8 * mib,
     )
-    same = exchange(normed, groups)
-    other = lax.ppermute(same, "wide", swap)
     own, sent = call(
         functools.partial(ffn_kernel, 512, 512),
         [shaped((half, width), f32), shaped((half, width), bf16)],
-        (same, other, gate_near, up_near, down_near),
+        (same, other, gate_near, up_near, down_near, route),
         20 * mib,
         scratch=[
             VMEM((rows, width), bf16),
@@ -252,6 +268,7 @@
         shaped((n, capacity, width + LANES), bf16),
         (parts, hidden_in, final_gain[None], route),
         16 * mib,
+        cost=ahead(codes),
     )
     recv = exchange(queries)
     scores = call(
@@ -259,7 +276,7 @@
         shaped((n, capacity, list_rows), f32),
         (recv, codes_near, jnp.swapaxes(scales, 1, 2)),
         20 * mib,
-        scratch=[VMEM((n * capacity, width + LANES), bf16)],
+        scratch=[VMEM((2 * n * capacity, width), bf16)],
     )
     back = exchange(scores)
     return call(best_kernel, shaped((q_dev, K_TOP), f32), (back, route), 8 * mib)

time: 92 us -> 68.5 us (0.74)
  blocking collectives: 39 us -> 52.3 us
  local copies, waits for them, and re-layouts: 14.1 us -> 1.52 us
  Pallas kernels: 22.5 us -> 11.5 us
  waiting for transfers between devices: 11.9 us -> 2.58 us
  starting transfers between devices: 3.79 us -> 0.2 us
    all_to_all x3 -> x4, blocking collectives: 39 us -> 52.3 us  [exchange(): lax.all_to_all(x, 'wide', 0, 0, axis_index_groups=axis_index_groups, tile...]
    unnamed x24 -> x26, local copies, waits for them, and re-layouts: 14.1 us -> 1.52 us
    pallas_call x7, Pallas kernels: 22.5 us -> 11.5 us  [call(): pl.pallas_call(kernel, out_shape=out_shape, in_specs=[pl.BlockSpec(memory...]
    all_to_all x1 -> x0, waiting for transfers between devices: 8.93 us -> none  [exchange(): lax.all_to_all(x, 'wide', 0, 0, axis_index_groups=axis_index_groups, tile...]
    all_to_all x1 -> x0, starting transfers between devices: 3.59 us -> none  [exchange(): lax.all_to_all(x, 'wide', 0, 0, axis_index_groups=axis_index_groups, tile...]
  transfers between devices with their start and end apart: 3 -> 2, of which waited for: 3 -> 2; matrix products, arithmetic and copies ran while one was open for 0% -> 0% of each run, Pallas kernels for 0% -> 0%
where the time goes in v2:
time: 68.5 us; the launch traced here: 68.2 us
  blocking collectives  52.3 us (76%)
  Pallas kernels  11.5 us (17%)
  waiting for transfers between devices  2.58 us (4%)
  local copies, waits for them, and re-layouts  1.52 us (2%)
    all_to_all x4, blocking collectives, exchange(): lax.all_to_all(x, 'wide', 0, 0, axis_index_groups=axis_index_groups, tile...  52.3 us
    pallas_call x7, Pallas kernels, call(): pl.pallas_call(kernel, out_shape=out_shape, in_specs=[pl.BlockSpec(memory...  11.5 us
    unnamed x26, local copies, waits for them, and re-layouts  1.52 us
    ppermute x1, waiting for transfers between devices, body(): came = lax.ppermute(sent, 'wide', swap)  1.4 us
  transfers between devices with their start and end apart: 2, of which 2 were waited for; matrix products, arithmetic and copies ran while one was open for 0% of the time, Pallas kernels for 0%

profile of v2, /device:TPU:0, one launch (start us, length us, event | category | flops | bytes accessed | tf_op | source)
XLA Modules:
  0.0 68.2 jit_solution(2455187862732822576)
XLA Ops:
  0.0 0.8 %copy-done.7 = bf16[4,4096]{1,0:T(4,128)(2,1)S(1)} copy-done((bf16[4,4096]{1,0:T(4,128)(2,1)S(1)}, bf16[4,4096]{1,0:T(4,128)(2,1)}, u32[]{:S(2)}) %copy-start.7) | copy-done | bytes 32792
  0.8 0.7 %copy-done.9 = f32[4096]{0:T(1024)S(1)} copy-done((f32[4096]{0:T(1024)S(1)}, f32[4096]{0:T(1024)}, u32[]{:S(2)}) %copy-start.9) | copy-done | bytes 16408
  1.5 0.0 copy-start.1
  1.5 0.0 copy-start.2
  1.5 0.1 shard_map.109
  1.7 16.3 %all_to_all.20.after_ref.same_ref = bf16[8,4,4096]{2,1,0:T(4,128)(2,1)S(1)} all-to-all(bf16[8,4,4096]{2,1,0:T(4,128)(2,1)S(1)} %shard_map.109), channel_id=1, replica_groups={{0,2,4,6,8,10,12,14},{1,3,5,7,9,11,13,15},{16,18,20,22,24,26,28,30},{17..., dimensions={0} | all-to-all | bytes 524288 | tf_op jit(solution)/shard_map/all_to_all | solution.py:230
  17.9 0.0 collective-permute-start
  18.0 0.0 copy-done.6
  18.0 0.3 shard_map.110.after_ref.route_ref
  18.3 0.0 copy-start.8
  18.3 0.0 copy-start.10
  18.3 1.2 %collective-permute-done.other_ref = bf16[8,4,4096]{2,1,0:T(4,128)(2,1)S(1)} collective-permute-done((bf16[8,4,4096]{2,1,0:T(4,128)(2,1)S(1)}, bf16[8,4,4096]{2,1,0:T(4,128)(2,1)S(1)}, u32[]{:S(2)}, u32[]{:S(2)}) %collective-permute-start) | collective-permute-done | bytes 262176 | tf_op jit(solution)/shard_map/ppermute | solution.py:244
  19.5 6.0 %shard_map.111 = (f32[32,4096]{1,0:T(8,128)S(1)}, bf16[32,4096]{1,0:T(8,128)(2,1)S(1)}) custom-call(bf16[8,4,4096]{2,1,0:T(4,128)(2,1)S(1)} %all_to_all.20.after_ref.same_ref, bf16[8,4,4096]{2,1,0:T(4,128)(2,1)S(1)} %collective-permute-done.other_ref, bf16[4096,896]{1,0:T(8,128)(2,1)S(1)} %copy-done, bf16[4096,896]{1,0:T(8,128)(2,1)S(1)} %copy-done.1, ...), custom_call_target="tpu_custom_call" | custom-call | tf_op jit(solution)/shard_map/pallas_call | solution.py:22
  25.5 0.2 collective-permute-start.1
  25.7 1.4 %collective-permute-done.1.came_ref = bf16[32,4096]{1,0:T(8,128)(2,1)S(1)} collective-permute-done((bf16[32,4096]{1,0:T(8,128)(2,1)S(1)}, bf16[32,4096]{1,0:T(8,128)(2,1)S(1)}, u32[]{:S(2)}, u32[]{:S(2)}) %collective-permute-start.1) | collective-permute-done | bytes 262176 | tf_op jit(solution)/shard_map/ppermute | solution.py:263
  27.1 0.1 shard_map.112
  27.1 12.9 %all_to_all.21.parts_ref = bf16[8,4,4096]{2,1,0:T(4,128)(2,1)S(1)} all-to-all(bf16[8,4,4096]{2,1,0:T(4,128)(2,1)S(1)} %shard_map.112), channel_id=1, replica_groups={{0,2,4,6,8,10,12,14},{1,3,5,7,9,11,13,15},{16,18,20,22,24,26,28,30},{17..., dimensions={0} | all-to-all | bytes 524288 | tf_op jit(solution)/shard_map/all_to_all | solution.py:230
  40.0 0.3 shard_map.113
  40.4 13.9 %all_to_all.22.came_ref = bf16[16,2,4224]{2,1,0:T(2,128)(2,1)S(1)} all-to-all(bf16[16,2,4224]{2,1,0:T(2,128)(2,1)S(1)} %shard_map.113), channel_id=1, replica_groups=mesh['grp'=2,'wide'=16] {'wide'}, dimensions={0} | all-to-all | bytes 540672 | tf_op jit(solution)/shard_map/all_to_all | solution.py:230
  54.3 0.0 slice-done
  54.3 0.0 copy-done.3
  54.3 3.3 %shard_map.114 = f32[16,2,128]{2,1,0:T(2,128)S(1)} custom-call(bf16[16,2,4224]{2,1,0:T(2,128)(2,1)S(1)} %all_to_all.22.came_ref, bf16[8,128,4096]{2,1,0:T(8,128)(2,1)S(1)} %bitcast.6, f32[8,32,128]{2,1,0:T(8,128)S(1)} %bitcast.7), custom_call_target="tpu_custom_call" | custom-call | tf_op jit(solution)/shard_map/pallas_call | solution.py:22
  57.6 9.2 %all_to_all.23.back_ref = f32[16,2,128]{2,1,0:T(2,128)S(1)} all-to-all(f32[16,2,128]{2,1,0:T(2,128)S(1)} %shard_map.114), channel_id=1, replica_groups=mesh['grp'=2,'wide'=16] {'wide'}, dimensions={0} | all-to-all | bytes 32768 | tf_op jit(solution)/shard_map/all_to_all | solution.py:230
  66.8 1.4 %shard_map.115 = f32[4,8]{1,0:T(4,128)} custom-call(f32[16,2,128]{2,1,0:T(2,128)S(1)} %all_to_all.23.back_ref, s32[32,128]{1,0:T(8,128)S(1)} %shard_map.110.after_ref.route_ref), custom_call_target="tpu_custom_call" | custom-call | tf_op jit(solution)/shard_map/pallas_call | solution.py:22
  (18 shorter events, 0.0 us)
Async XLA Ops:
  0.0 0.8 %copy-start.7 = (bf16[4,4096]{1,0:T(4,128)(2,1)S(1)}, bf16[4,4096]{1,0:T(4,128)(2,1)}, u32[]{:S(2)}) copy-start(bf16[4,4096]{1,0:T(4,128)(2,1)} %hidden_ref.3) | copy-start | bytes 98308
  0.8 0.7 %copy-start.9 = (f32[4096]{0:T(1024)S(1)}, f32[4096]{0:T(1024)}, u32[]{:S(2)}) copy-start(f32[4096]{0:T(1024)} %param.12) | copy-start | bytes 49156
  1.5 16.5 %copy-start.4 = (s32[4,8]{1,0:T(4,128)S(1)}, s32[4,8]{1,0:T(4,128)}, u32[]{:S(2)}) copy-start(s32[4,8]{1,0:T(4,128)} %probes_ref.1) | copy-start | bytes 388
  1.5 16.5 %copy-start.5 = (s32[128]{0:T(128)S(1)}, s32[128]{0:T(128)}, u32[]{:S(2)}) copy-start(s32[128]{0:T(128)} %param.20) | copy-start | bytes 1540
  1.5 16.5 %copy-start.6 = (s32[128]{0:T(128)S(1)}, s32[128]{0:T(128)}, u32[]{:S(2)}) copy-start(s32[128]{0:T(128)} %param.19) | copy-start | bytes 1540
  1.5 18.0 %copy-start = (bf16[4096,896]{1,0:T(8,128)(2,1)S(1)}, bf16[4096,896]{1,0:T(8,128)(2,1)}, u32[]{:S(2)}) copy-start(bf16[4096,896]{1,0:T(8,128)(2,1)} %gate_ref.1) | copy-start | bytes 22020100
  1.5 18.0 %copy-start.1 = (bf16[4096,896]{1,0:T(8,128)(2,1)S(1)}, bf16[4096,896]{1,0:T(8,128)(2,1)}, u32[]{:S(2)}) copy-start(bf16[4096,896]{1,0:T(8,128)(2,1)} %up_ref.1) | copy-start | bytes 22020100
  1.5 18.0 %copy-start.2 = (bf16[896,4096]{1,0:T(8,128)(2,1)S(1)}, bf16[896,4096]{1,0:T(8,128)(2,1)}, u32[]{:S(2)}) copy-start(bf16[896,4096]{1,0:T(8,128)(2,1)} %down_ref.1) | copy-start | bytes 22020100
  17.9 1.5 %collective-permute-start = (bf16[8,4,4096]{2,1,0:T(4,128)(2,1)S(1)}, bf16[8,4,4096]{2,1,0:T(4,128)(2,1)S(1)}, u32[]{:S(2)}, u32[]{:S(2)}) collective-permute-start(bf16[8,4,4096]{2,1,0:T(4,128)(2,1)S(1)} %all_to_all.20.after_ref.same_ref), channel_id=1, source_target_pairs={{0,1},{1,0},{2,3},{3,2},{4,5},{5,4},{6,7},{7,6},{8,9},{9,8},{10,11... | collective-permute-start | bytes 786440 | tf_op jit(solution)/shard_map/ppermute | solution.py:244
  18.3 21.7 %copy-start.8 = (bf16[4,4096]{1,0:T(4,128)(2,1)S(1)}, bf16[4,4096]{1,0:T(4,128)(2,1)}, u32[]{:S(2)}) copy-start(bf16[4,4096]{1,0:T(4,128)(2,1)} %hidden_ref.3) | copy-start | bytes 98308
  18.3 21.7 %copy-start.10 = (f32[4096]{0:T(1024)S(1)}, f32[4096]{0:T(1024)}, u32[]{:S(2)}) copy-start(f32[4096]{0:T(1024)} %param.16) | copy-start | bytes 49156
  25.5 1.6 %collective-permute-start.1 = (bf16[32,4096]{1,0:T(8,128)(2,1)S(1)}, bf16[32,4096]{1,0:T(8,128)(2,1)S(1)}, u32[]{:S(2)}, u32[]{:S(2)}) collective-permute-start(bf16[32,4096]{1,0:T(8,128)(2,1)S(1)} %get-tuple-element.8), channel_id=1, source_target_pairs={{0,1},{1,0},{2,3},{3,2},{4,5},{5,4},{6,7},{7,6},{8,9},{9,8},{10,11... | collective-permute-start | bytes 786440 | tf_op jit(solution)/shard_map/ppermute | solution.py:263
  27.1 27.2 %slice-start = ((s8[8388608]{0:T(1024)(128)(4,1)}), s8[4194304]{0:T(1024)(128)(4,1)S(1)}, s32[]{:S(2)}) async-start(s8[8388608]{0:T(1024)(128)(4,1)} %bitcast.5), calls=%async_computation.4 | async-start | bytes 8388608
  40.0 14.3 %slice-start.1 = ((s8[8388608]{0:T(1024)(128)(4,1)}), s8[4194304]{0:T(1024)(128)(4,1)S(1)}, s32[]{:S(2)}) async-start(s8[8388608]{0:T(1024)(128)(4,1)} %bitcast.5), calls=%async_computation.5 | async-start | bytes 8388608
  40.0 14.3 %copy-start.3 = (f32[8,128,32]{1,2,0:T(8,128)S(1)}, f32[8,128,32]{1,2,0:T(8,128)}, u32[]{:S(2)}) copy-start(f32[8,128,32]{1,2,0:T(8,128)} %param.18) | copy-start | bytes 393220

commit v3 on v2

--- a/solution.py
+++ b/solution.py
@@ -37,16 +37,31 @@
     return pl.CostEstimate(flops=1000 * total, bytes_accessed=1 << 20, transcendentals=0)
 
 
+def products(count):
+    return pl.CostEstimate(flops=2 * count, bytes_accessed=1 << 20, transcendentals=0)
+
+
 def shaped(shape, dtype):
     return jax.ShapeDtypeStruct(shape, dtype)
 
 
-def norm_kernel(hidden_ref, gain_ref, out_ref):
-    rows = hidden_ref[...].astype(jnp.float32)
+def norm_kernel(hidden_ref, gain_ref, out_ref, rows_ref, scale_ref, sems):
+    rows_copy = pltpu.make_async_copy(hidden_ref, rows_ref, sems.at[0])
+    gain_copy = pltpu.make_async_copy(gain_ref, scale_ref, sems.at[1])
+    rows_copy.start()
+    gain_copy.start()
+    rows_copy.wait()
+    gain_copy.wait()
+    rows = rows_ref[...].astype(jnp.float32)
     scale = lax.rsqrt(jnp.mean(rows * rows, axis=-1, keepdims=True) + 1e-05)
-    normed = (rows * scale * gain_ref[...]).astype(jnp.bfloat16)
+    out_ref[...] = (rows * scale * scale_ref[...]).astype(jnp.bfloat16)
+
+
+def spread_kernel(normed_ref, out_ref):
+    half = out_ref.shape[2]
     for k in range(out_ref.shape[0]):
-        out_ref[k] = normed
+        core = k % 2
+        out_ref[k] = normed_ref[:, core * half : (core + 1) * half]
 
 
 def route_kernel(lists_dev, capacity, probes_ref, slot_ref, count_ref, after_ref, out_ref):
@@ -90,33 +105,40 @@
     out_ref[...] = jnp.where(place == 2, of_slot(as_row(valid)), out)
 
 
-def ffn_kernel(
-    k_chunk, n_chunk, same_ref, other_ref, gate_ref, up_ref, down_ref, after_ref, own_ref, send_ref,
-    rows_ref, gate_acc, up_acc, act_ref,
+def half_span(mine, half):
+    core = lax.rem(lax.axis_index("wide"), 2)
+    which = core if mine else 1 - core
+    return pl.ds(pl.multiple_of(which * half, half), half)
+
+
+def first_kernel(here_ref, gate_ref, up_ref, after_ref, gate_out, up_out, rows_ref):
+    rows_ref[...] = here_ref[...].reshape(rows_ref.shape)
+    span = half_span(True, rows_ref.shape[1])
+    gate_out[...] = jnp.dot(rows_ref[...], gate_ref[span, :], preferred_element_type=jnp.float32)
+    up_out[...] = jnp.dot(rows_ref[...], up_ref[span, :], preferred_element_type=jnp.float32)
+
+
+def second_kernel(
+    there_ref, gate_part, up_part, gate_ref, up_ref, down_ref, after_ref, act_ref, send_ref, rows_ref
 ):
-    chips, q_dev, width = same_ref.shape
-    half = chips * q_dev
-    rows_ref[:half, :] = same_ref[...].reshape(half, width)
-    rows_ref[half:, :] = other_ref[...].reshape(half, width)
-    gate_acc[...] = jnp.zeros_like(gate_acc)
-    up_acc[...] = jnp.zeros_like(up_acc)
-
-    @pl.loop(0, width // k_chunk)
-    def _(step):
-        span = pl.ds(pl.multiple_of(step * k_chunk, k_chunk), k_chunk)
-        x = rows_ref[:, span]
-        gate_acc[...] += jnp.dot(x, gate_ref[span, :], preferred_element_type=jnp.float32)
-        up_acc[...] += jnp.dot(x, up_ref[span, :], preferred_element_type=jnp.float32)
-
-    gate = gate_acc[...]
-    act_ref[...] = (gate / (1.0 + jnp.exp(-gate)) * up_acc[...]).astype(jnp.bfloat16)
-
-    @pl.loop(0, width // n_chunk)
-    def _(step):
-        span = pl.ds(pl.multiple_of(step * n_chunk, n_chunk), n_chunk)
-        out = jnp.dot(act_ref[...], down_ref[:, span], preferred_element_type=jnp.float32)
-        own_ref[:, span] = out[:half]
-        send_ref[:, span] = out[half:].astype(jnp.bfloat16)
+    half = rows_ref.shape[1]
+    rows_ref[...] = there_ref[...].reshape(rows_ref.shape)
+    span = half_span(False, half)
+    gate = gate_part[...] + jnp.dot(
+        rows_ref[...], gate_ref[span, :], preferred_element_type=jnp.float32
+    )
+    up = up_part[...] + jnp.dot(
+        rows_ref[...], up_ref[span, :], preferred_element_type=jnp.float32
+    )
+    act_ref[...] = (gate / (1.0 + jnp.exp(-gate)) * up).astype(jnp.bfloat16)
+    send_ref[...] = jnp.dot(
+        act_ref[...], down_ref[:, span], preferred_element_type=jnp.float32
+    ).astype(jnp.bfloat16)
+
+
+def third_kernel(act_ref, down_ref, own_ref):
+    span = half_span(True, own_ref.shape[1])
+    own_ref[...] = jnp.dot(act_ref[...], down_ref[:, span], preferred_element_type=jnp.float32)
 
 
 def add_kernel(own_ref, came_ref, out_ref):
@@ -125,10 +147,12 @@
 
 
 def embed_kernel(parts_ref, hidden_ref, gain_ref, route_ref, out_ref):
-    chips, q_dev, width = parts_ref.shape
-    total = parts_ref[0].astype(jnp.float32)
-    for k in range(1, chips):
-        total += parts_ref[k].astype(jnp.float32)
+    devices, q_dev, half = parts_ref.shape
+    width = 2 * half
+    totals = [parts_ref[core].astype(jnp.float32) for core in range(2)]
+    for k in range(2, devices):
+        totals[k % 2] += parts_ref[k].astype(jnp.float32)
+    total = jnp.concatenate(totals, axis=1)
     scaled = gain_ref[...] * (hidden_ref[...].astype(jnp.float32) + total)
     embedded = scaled * lax.rsqrt(jnp.sum(scaled * scaled, axis=-1, keepdims=True) + 1e-06)
     query = route_ref[:, 0:1]
@@ -154,24 +178,22 @@
         rows_ref[(1 - kept) * pairs : (2 - kept) * pairs, span] = nothing
     local = came[:, width : width + 1].astype(jnp.float32).astype(jnp.int32)
 
-    def two_lists(index, picked):
-        first = index * 2
+    picked = jnp.zeros((pairs, list_rows), jnp.float32)
+    for first in range(0, lists, 2):
         scale = jnp.concatenate([scales_ref[first], scales_ref[first + 1]], axis=1)
         total = jnp.zeros((pairs, 2 * list_rows), jnp.float32)
         for step in range(width // (2 * BLOCK)):
             span = slice(step * 2 * BLOCK, (step + 1) * 2 * BLOCK)
             part = lax.dot_general(
                 rows_ref[:, span],
-                codes_ref[pl.ds(first, 2), :, span].reshape(2 * list_rows, 2 * BLOCK),
+                codes_ref[first : first + 2, :, span].reshape(2 * list_rows, 2 * BLOCK),
                 (((1,), (1,)), ((), ())),
                 preferred_element_type=jnp.float32,
             )
             total += part[:pairs] * scale[2 * step : 2 * step + 1, :]
             total += part[pairs:] * scale[2 * step + 1 : 2 * step + 2, :]
         picked = jnp.where(local == first, total[:, :list_rows], picked)
-        return jnp.where(local == first + 1, total[:, list_rows:], picked)
-
-    picked = lax.fori_loop(0, lists // 2, two_lists, jnp.zeros((pairs, list_rows), jnp.float32))
+        picked = jnp.where(local == first + 1, total[:, list_rows:], picked)
     out_ref[...] = picked.reshape(out_ref.shape)
 
 
@@ -216,53 +238,77 @@
     q_dev, width = hidden_in.shape
     hidden_units = gate_weight.shape[1]
     n = lax.axis_size("wide")
-    chips = n // 2
-    half = chips * q_dev
-    rows = 2 * half
+    half = width // 2
+    rows = n * q_dev
     lists_dev, list_rows, _ = codes.shape
     capacity = (q_dev * PROBES + n - 1) // n
-    groups = [[core + 2 * k for k in range(chips)] for core in range(2)]
     swap = [(i, i ^ 1) for i in range(n)]
     mib = 1 << 20
     f32, bf16 = jnp.float32, jnp.bfloat16
 
-    def exchange(x, axis_index_groups=None):
-        return lax.all_to_all(
-            x, "wide", 0, 0, axis_index_groups=axis_index_groups, tiled=True
-        )
+    def exchange(x):
+        return lax.all_to_all(x, "wide", 0, 0, tiled=True)
 
     gate_near = pltpu.with_memory_space_constraint(gate_weight, VMEM)
     up_near = pltpu.with_memory_space_constraint(up_weight, VMEM)
     down_near = pltpu.with_memory_space_constraint(down_weight, VMEM)
     codes_near = pltpu.with_memory_space_constraint(codes, VMEM)
 
-    normed = call(
-        norm_kernel, shaped((chips, q_dev, width), bf16), (hidden_in, ffn_gain[None]), 8 * mib,
+    normed = pl.pallas_call(
+        norm_kernel,
+        out_shape=shaped((q_dev, width), bf16),
+        in_specs=[pl.BlockSpec(memory_space=pltpu.HBM)] * 2,
+        out_specs=pl.BlockSpec(memory_space=VMEM),
+        scratch_shapes=[
+            VMEM((q_dev, width), bf16),
+            VMEM((1, width), f32),
+            pltpu.SemaphoreType.DMA((2,)),
+        ],
+        compiler_params=pltpu.CompilerParams(vmem_limit_bytes=8 * mib),
+    )(
+        pltpu.with_memory_space_constraint(hidden_in, pltpu.HBM),
+        pltpu.with_memory_space_constraint(ffn_gain[None], pltpu.HBM),
+    )
+    spread = call(
+        spread_kernel,
+        shaped((n, q_dev, half), bf16),
+        (normed,),
+        8 * mib,
         cost=ahead(gate_weight, up_weight, down_weight),
     )
-    same = exchange(normed, groups)
-    other = lax.ppermute(same, "wide", swap)
+    here = exchange(spread)
+    there = lax.ppermute(here, "wide", swap)
     route = call(
         functools.partial(route_kernel, lists_dev, capacity),
         shaped((n * capacity, LANES), jnp.int32),
-        (probes, list_slot[None], counts[None], same),
-        8 * mib,
-    )
-    own, sent = call(
-        functools.partial(ffn_kernel, 512, 512),
-        [shaped((half, width), f32), shaped((half, width), bf16)],
-        (same, other, gate_near, up_near, down_near, route),
-        20 * mib,
-        scratch=[
-            VMEM((rows, width), bf16),
-            VMEM((rows, hidden_units), f32),
-            VMEM((rows, hidden_units), f32),
-            VMEM((rows, hidden_units), bf16),
-        ],
+        (probes, list_slot[None], counts[None], here),
+        8 * mib,
+    )
+    gate_part, up_part = call(
+        first_kernel,
+        [shaped((rows, hidden_units), f32)] * 2,
+        (here, gate_near, up_near, down_near),
+        8 * mib,
+        cost=products(rows * half * hidden_units * 2),
+        scratch=[VMEM((rows, half), bf16)],
+    )
+    act, sent = call(
+        second_kernel,
+        [shaped((rows, hidden_units), bf16), shaped((rows, half), bf16)],
+        (there, gate_part, up_part, gate_near, up_near, down_near, route),
+        8 * mib,
+        scratch=[VMEM((rows, half), bf16)],
     )
     came = lax.ppermute(sent, "wide", swap)
-    pairs_sum = call(add_kernel, shaped((chips, q_dev, width), bf16), (own, came), 16 * mib)
-    parts = exchange(pairs_sum, groups)
+    own = call(
+        third_kernel,
+        shaped((rows, half), f32),
+        (act, down_near),
+        8 * mib,
+        cost=products(rows * half * hidden_units),
+    )
+    pairs_sum = call(add_kernel, shaped((n, q_dev, half), bf16), (own, came), 16 * mib)
+    parts = exchange(pairs_sum)
     queries = call(
         embed_kernel,
         shaped((n, capacity, width + LANES), bf16),

time: 68.5 us -> 64.2 us (0.937)
  waiting for transfers between devices: 2.58 us -> 0.4 us
  Pallas kernels: 11.5 us -> 9.97 us
  local copies, waits for them, and re-layouts: 1.52 us -> 0.06 us
    pallas_call x7 -> x9, Pallas kernels: 11.5 us -> 9.06 us  [call(): pl.pallas_call(kernel, out_shape=out_shape, in_specs=[pl.BlockSpec(memory...]
    unnamed x26 -> x22, local copies, waits for them, and re-layouts: 1.52 us -> 0.06 us
    ppermute x1, waiting for transfers between devices: 1.18 us -> 0.01 us  [body(): there = lax.ppermute(here, 'wide', swap)]
    ppermute x1, waiting for transfers between devices: 1.4 us -> 0.4 us  [body(): came = lax.ppermute(sent, 'wide', swap)]
    pallas_call x0 -> x1, Pallas kernels: none -> 0.91 us  [body(): pl.pallas_call(norm_kernel, out_shape=shaped((q_dev, width), bf16), in_sp...]
  transfers between devices with their start and end apart: 2 -> 2, of which waited for: 2 -> 1; matrix products, arithmetic and copies ran while one was open for 0% -> 0% of each run, Pallas kernels for 0% -> 4%
where the time goes in v3:
time: 64.2 us; the launch traced here: 63.8 us
  blocking collectives  52.6 us (82%)
  Pallas kernels  9.97 us (16%)
    all_to_all x4, blocking collectives, exchange(): return lax.all_to_all(x, 'wide', 0, 0, tiled=True)  52.6 us
    pallas_call x9, Pallas kernels, call(): pl.pallas_call(kernel, out_shape=out_shape, in_specs=[pl.BlockSpec(memory...  9.06 us
  transfers between devices with their start and end apart: 2, of which 1 were waited for; matrix products, arithmetic and copies ran while one was open for 0% of the time, Pallas kernels for 4%

profile of v3, /device:TPU:0, one launch (start us, length us, event | category | flops | bytes accessed | tf_op | source)
XLA Modules:
  0.0 63.8 jit_solution(1469848356755731326)
XLA Ops:
  0.0 0.9 %shard_map.109.normed_ref = bf16[4,4096]{1,0:T(4,128)(2,1)S(1)} custom-call(bf16[4,4096]{1,0:T(4,128)(2,1)} %hidden_ref.3, f32[1,4096]{1,0:T(1,128)} %bitcast.11), custom_call_target="tpu_custom_call" | custom-call | tf_op jit(solution)/shard_map/pallas_call | solution.py:257
  0.9 0.0 copy-start.5
  0.9 0.0 copy-start.6
  0.9 0.0 copy-start.7
  1.0 0.0 copy-start
  1.0 0.0 copy-start.1
  1.0 0.0 copy-start.2
  1.0 17.5 %all_to_all.20.here_ref.after_ref = bf16[16,4,2048]{2,1,0:T(4,128)(2,1)S(1)} all-to-all(bf16[16,4,2048]{2,1,0:T(4,128)(2,1)S(1)} %shard_map.110), channel_id=1, replica_groups=mesh['grp'=2,'wide'=16] {'wide'}, dimensions={0} | all-to-all | bytes 524288 | tf_op jit(solution)/shard_map/all_to_all | solution.py:250
  18.5 0.0 collective-permute-start
  18.5 0.3 shard_map.112.after_ref.route_ref
  18.9 1.4 %shard_map.111 = (f32[64,896]{1,0:T(8,128)S(1)}, f32[64,896]{1,0:T(8,128)S(1)}) custom-call(bf16[16,4,2048]{2,1,0:T(4,128)(2,1)S(1)} %all_to_all.20.here_ref.after_ref, bf16[4096,896]{1,0:T(8,128)(2,1)S(1)} %copy-done.1, bf16[4096,896]{1,0:T(8,128)(2,1)S(1)} %copy-done.2, bf16[896,4096]{1,0:T(8,128)(2,1)S(1)} %copy-done), custom_call_target="tpu_custom_call" | custom-call | flops 469762048 | bytes 1048576 | tf_op jit(solution)/shard_map/pallas_call | solution.py:22
  20.2 2.0 %shard_map.113 = (bf16[64,896]{1,0:T(8,128)(2,1)S(1)}, bf16[64,2048]{1,0:T(8,128)(2,1)S(1)}) custom-call(bf16[16,4,2048]{2,1,0:T(4,128)(2,1)S(1)} %collective-permute-done.there_ref, f32[64,896]{1,0:T(8,128)S(1)} %get-tuple-element.9.gate_part, f32[64,896]{1,0:T(8,128)S(1)} %get-tuple-element.10.up_part, bf16[4096,896]{1,0:T(8,128)(2,1)S(1)} %copy-done.1, ...), custom_call_target="tpu_custom_call" | custom-call | tf_op jit(solution)/shard_map/pallas_call | solution.py:22
  22.3 0.0 copy-start.4
  22.3 0.0 copy-start.8
  22.3 0.6 collective-permute-start.1
  22.9 0.8 %shard_map.114.own_ref = f32[64,2048]{1,0:T(8,128)S(1)} custom-call(bf16[64,896]{1,0:T(8,128)(2,1)S(1)} %get-tuple-element.11.act_ref, bf16[896,4096]{1,0:T(8,128)(2,1)S(1)} %copy-done), custom_call_target="tpu_custom_call" | custom-call | flops 234881024 | bytes 1048576 | tf_op jit(solution)/shard_map/pallas_call | solution.py:22
  23.6 0.4 collective-permute-done.1.came_ref
  24.0 0.1 shard_map.115
  24.1 12.8 %all_to_all.21.parts_ref = bf16[16,4,2048]{2,1,0:T(4,128)(2,1)S(1)} all-to-all(bf16[16,4,2048]{2,1,0:T(4,128)(2,1)S(1)} %shard_map.115), channel_id=1, replica_groups=mesh['grp'=2,'wide'=16] {'wide'}, dimensions={0} | all-to-all | bytes 524288 | tf_op jit(solution)/shard_map/all_to_all | solution.py:250
  36.9 0.3 shard_map.116
  37.3 13.1 %all_to_all.22.came_ref = bf16[16,2,4224]{2,1,0:T(2,128)(2,1)S(1)} all-to-all(bf16[16,2,4224]{2,1,0:T(2,128)(2,1)S(1)} %shard_map.116), channel_id=1, replica_groups=mesh['grp'=2,'wide'=16] {'wide'}, dimensions={0} | all-to-all | bytes 540672 | tf_op jit(solution)/shard_map/all_to_all | solution.py:250
  50.4 2.8 %shard_map.117 = f32[16,2,128]{2,1,0:T(2,128)S(1)} custom-call(bf16[16,2,4224]{2,1,0:T(2,128)(2,1)S(1)} %all_to_all.22.came_ref, bf16[8,128,4096]{2,1,0:T(8,128)(2,1)S(1)} %bitcast.6, f32[8,32,128]{2,1,0:T(8,128)S(1)} %bitcast.7), custom_call_target="tpu_custom_call" | custom-call | tf_op jit(solution)/shard_map/pallas_call | solution.py:22
  53.2 9.2 %all_to_all.23.back_ref = f32[16,2,128]{2,1,0:T(2,128)S(1)} all-to-all(f32[16,2,128]{2,1,0:T(2,128)S(1)} %shard_map.117), channel_id=1, replica_groups=mesh['grp'=2,'wide'=16] {'wide'}, dimensions={0} | all-to-all | bytes 32768 | tf_op jit(solution)/shard_map/all_to_all | solution.py:250
  62.4 1.4 %shard_map.118 = f32[4,8]{1,0:T(4,128)} custom-call(f32[16,2,128]{2,1,0:T(2,128)S(1)} %all_to_all.23.back_ref, s32[32,128]{1,0:T(8,128)S(1)} %shard_map.112.after_ref.route_ref), custom_call_target="tpu_custom_call" | custom-call | tf_op jit(solution)/shard_map/pallas_call | solution.py:22
  (17 shorter events, 0.1 us)
Async XLA Ops:
  0.9 17.6 %copy-start.5 = (s32[4,8]{1,0:T(4,128)S(1)}, s32[4,8]{1,0:T(4,128)}, u32[]{:S(2)}) copy-start(s32[4,8]{1,0:T(4,128)} %probes_ref.1) | copy-start | bytes 388
  0.9 17.6 %copy-start.6 = (s32[128]{0:T(128)S(1)}, s32[128]{0:T(128)}, u32[]{:S(2)}) copy-start(s32[128]{0:T(128)} %param.20) | copy-start | bytes 1540
  0.9 17.6 %copy-start.7 = (s32[128]{0:T(128)S(1)}, s32[128]{0:T(128)}, u32[]{:S(2)}) copy-start(s32[128]{0:T(128)} %param.19) | copy-start | bytes 1540
  1.0 17.9 %copy-start = (bf16[896,4096]{1,0:T(8,128)(2,1)S(1)}, bf16[896,4096]{1,0:T(8,128)(2,1)}, u32[]{:S(2)}) copy-start(bf16[896,4096]{1,0:T(8,128)(2,1)} %down_ref.3) | copy-start | bytes 22020100
  1.0 17.9 %copy-start.1 = (bf16[4096,896]{1,0:T(8,128)(2,1)S(1)}, bf16[4096,896]{1,0:T(8,128)(2,1)}, u32[]{:S(2)}) copy-start(bf16[4096,896]{1,0:T(8,128)(2,1)} %gate_ref.3) | copy-start | bytes 22020100
  1.0 17.9 %copy-start.2 = (bf16[4096,896]{1,0:T(8,128)(2,1)S(1)}, bf16[4096,896]{1,0:T(8,128)(2,1)}, u32[]{:S(2)}) copy-start(bf16[4096,896]{1,0:T(8,128)(2,1)} %up_ref.3) | copy-start | bytes 22020100
  18.5 1.7 %collective-permute-start = (bf16[16,4,2048]{2,1,0:T(4,128)(2,1)S(1)}, bf16[16,4,2048]{2,1,0:T(4,128)(2,1)S(1)}, u32[]{:S(2)}, u32[]{:S(2)}) collective-permute-start(bf16[16,4,2048]{2,1,0:T(4,128)(2,1)S(1)} %all_to_all.20.here_ref.after_ref), channel_id=1, source_target_pairs={{0,1},{1,0},{2,3},{3,2},{4,5},{5,4},{6,7},{7,6},{8,9},{9,8},{10,11... | collective-permute-start | bytes 786440 | tf_op jit(solution)/shard_map/ppermute | solution.py:280
  22.3 14.7 %copy-start.4 = (bf16[4,4096]{1,0:T(4,128)(2,1)S(1)}, bf16[4,4096]{1,0:T(4,128)(2,1)}, u32[]{:S(2)}) copy-start(bf16[4,4096]{1,0:T(4,128)(2,1)} %hidden_ref.3) | copy-start | bytes 98308
  22.3 14.6 %copy-start.8 = (f32[4096]{0:T(1024)S(1)}, f32[4096]{0:T(1024)}, u32[]{:S(2)}) copy-start(f32[4096]{0:T(1024)} %param.16) | copy-start | bytes 49156
  22.3 1.7 %collective-permute-start.1 = (bf16[64,2048]{1,0:T(8,128)(2,1)S(1)}, bf16[64,2048]{1,0:T(8,128)(2,1)S(1)}, u32[]{:S(2)}, u32[]{:S(2)}) collective-permute-start(bf16[64,2048]{1,0:T(8,128)(2,1)S(1)} %get-tuple-element.12), channel_id=1, source_target_pairs={{0,1},{1,0},{2,3},{3,2},{4,5},{5,4},{6,7},{7,6},{8,9},{9,8},{10,11... | collective-permute-start | bytes 786440 | tf_op jit(solution)/shard_map/ppermute | solution.py:302
  22.9 27.5 %slice-start = ((s8[8388608]{0:T(1024)(128)(4,1)}), s8[4194304]{0:T(1024)(128)(4,1)S(1)}, s32[]{:S(2)}) async-start(s8[8388608]{0:T(1024)(128)(4,1)} %bitcast.5), calls=%async_computation.4 | async-start | bytes 8388608
  36.9 13.4 %slice-start.1 = ((s8[8388608]{0:T(1024)(128)(4,1)}), s8[4194304]{0:T(1024)(128)(4,1)S(1)}, s32[]{:S(2)}) async-start(s8[8388608]{0:T(1024)(128)(4,1)} %bitcast.5), calls=%async_computation.5 | async-start | bytes 8388608
  36.9 13.4 %copy-start.3 = (f32[8,128,32]{1,2,0:T(8,128)S(1)}, f32[8,128,32]{1,2,0:T(8,128)}, u32[]{:S(2)}) copy-start(f32[8,128,32]{1,2,0:T(8,128)} %param.18) | copy-start | bytes 393220

commit v4 on v3

--- a/solution.py
+++ b/solution.py
@@ -11,6 +11,7 @@
 K_TOP = 8
 BLOCK = 128
 LANES = 128
+DIGIT = 256
 
 floor_score = -1e30
 
@@ -45,23 +46,77 @@
     return jax.ShapeDtypeStruct(shape, dtype)
 
 
-def norm_kernel(hidden_ref, gain_ref, out_ref, rows_ref, scale_ref, sems):
-    rows_copy = pltpu.make_async_copy(hidden_ref, rows_ref, sems.at[0])
-    gain_copy = pltpu.make_async_copy(gain_ref, scale_ref, sems.at[1])
-    rows_copy.start()
-    gain_copy.start()
-    rows_copy.wait()
-    gain_copy.wait()
+def norm_kernel(hidden_ref, gain_ref, probes_ref, out_ref, rows_ref, scale_ref, ids_ref, sems):
+    copies = [
+        pltpu.make_async_copy(source, target, sems.at[index])
+        for index, (source, target) in enumerate(
+            [(hidden_ref, rows_ref), (gain_ref, scale_ref), (probes_ref, ids_ref)]
+        )
+    ]
+    for copy in copies:
+        copy.start()
+    for copy in copies:
+        copy.wait()
     rows = rows_ref[...].astype(jnp.float32)
+    width = rows.shape[1]
     scale = lax.rsqrt(jnp.mean(rows * rows, axis=-1, keepdims=True) + 1e-05)
-    out_ref[...] = (rows * scale * scale_ref[...]).astype(jnp.bfloat16)
+    out_ref[:, :width] = (rows * scale * scale_ref[...]).astype(jnp.bfloat16)
+
+    q_dev, probes = ids_ref.shape
+    pairs = q_dev * probes
+    lane = lax.broadcasted_iota(jnp.int32, (q_dev, LANES), 1)
+    query = lax.broadcasted_iota(jnp.int32, (q_dev, LANES), 0)
+    ids = jnp.zeros((q_dev, LANES), jnp.int32)
+    for j in range(probes):
+        ids = jnp.where(lane % probes == j, ids_ref[:, j : j + 1], ids)
+    ids = jnp.where((lane % pairs) // probes == query, ids, 0)
+    ids = jnp.sum(ids, axis=0, keepdims=True)
+    digits = jnp.where(lane < pairs, ids // DIGIT, ids % DIGIT)
+    digits = jnp.where(lane < 2 * pairs, digits, 0)
+    out_ref[:, width:] = digits.astype(jnp.float32).astype(jnp.bfloat16)
 
 
 def spread_kernel(normed_ref, out_ref):
-    half = out_ref.shape[2]
+    half = out_ref.shape[2] - LANES
     for k in range(out_ref.shape[0]):
         core = k % 2
-        out_ref[k] = normed_ref[:, core * half : (core + 1) * half]
+        out_ref[k, :, :half] = normed_ref[:, core * half : (core + 1) * half]
+        out_ref[k, :, half:] = normed_ref[:, 2 * half :]
+
+
+def wanted_kernel(capacity, q_dev, probes, here_ref, slot_ref, after_ref, out_ref):
+    devices, _, wide = here_ref.shape
+    half = wide - LANES
+    lists = slot_ref.shape[1]
+    pairs = q_dev * probes
+    lists_dev = lists // devices
+    me = lax.axis_index("wide")
+    tails = here_ref[:, :, half:].astype(jnp.float32)
+    tails = jnp.max(tails, axis=1).astype(jnp.int32)
+    ids = tails[:, :pairs] * DIGIT + tails[:, pairs : 2 * pairs]
+    number = lax.broadcasted_iota(jnp.int32, (1, lists), 1)
+    local = jnp.full((devices, pairs), -1, jnp.int32)
+    for index in range(lists_dev):
+        held = slot_ref[...] == me * lists_dev + index
+        mine = jnp.sum(jnp.where(held, number, 0), axis=1, keepdims=True)
+        local = jnp.where(ids == mine, index, local)
+    pair = lax.broadcasted_iota(jnp.int32, (devices, pairs), 1)
+    home = lax.broadcasted_iota(jnp.int32, (devices, 1), 0)
+    place = lax.broadcasted_iota(jnp.int32, (devices, LANES), 1)
+    side = lax.rem(me, 4) // 2
+    before = jnp.full((devices, 1), -1, jnp.int32)
+    for rank in range(capacity):
+        open_pair = (local >= 0) & (pair > before)
+        chosen = jnp.min(jnp.where(open_pair, pair, pairs), axis=1, keepdims=True)
+        there = jnp.sum(jnp.where(pair == chosen, local, 0), axis=1, keepdims=True)
+        row = jnp.where(
+            lax.rem(home, 4) // 2 == side, 0, devices * q_dev // 2
+        ) + home // 4 * (2 * q_dev) + lax.rem(home, 2) * q_dev + chosen // probes
+        row = jnp.where(chosen < pairs, row, -1)
+        out_ref[rank * devices : (rank + 1) * devices, :] = jnp.where(
+            place == 0, row, jnp.where(place == 1, there, 0)
+        )
+        before = chosen
 
 
 def route_kernel(lists_dev, capacity, probes_ref, slot_ref, count_ref, after_ref, out_ref):
@@ -112,17 +167,17 @@
 
 
 def first_kernel(here_ref, gate_ref, up_ref, after_ref, gate_out, up_out, rows_ref):
-    rows_ref[...] = here_ref[...].reshape(rows_ref.shape)
+    rows_ref[...] = here_ref[:, :, : rows_ref.shape[1]].reshape(rows_ref.shape)
     span = half_span(True, rows_ref.shape[1])
     gate_out[...] = jnp.dot(rows_ref[...], gate_ref[span, :], preferred_element_type=jnp.float32)
     up_out[...] = jnp.dot(rows_ref[...], up_ref[span, :], preferred_element_type=jnp.float32)
 
 
 def second_kernel(
-    there_ref, gate_part, up_part, gate_ref, up_ref, down_ref, after_ref, act_ref, send_ref, rows_ref
+    there_ref, gate_part, up_part, gate_ref, up_ref, down_ref, hidden_ref, act_ref, send_ref, rows_ref
 ):
     half = rows_ref.shape[1]
-    rows_ref[...] = there_ref[...].reshape(rows_ref.shape)
+    rows_ref[...] = there_ref[:, :, :half].reshape(rows_ref.shape)
     span = half_span(False, half)
     gate = gate_part[...] + jnp.dot(
         rows_ref[...], gate_ref[span, :], preferred_element_type=jnp.float32
@@ -131,9 +186,12 @@
         rows_ref[...], up_ref[span, :], preferred_element_type=jnp.float32
     )
     act_ref[...] = (gate / (1.0 + jnp.exp(-gate)) * up).astype(jnp.bfloat16)
-    send_ref[...] = jnp.dot(
+    rows = act_ref.shape[0]
+    send_ref[:rows, :] = jnp.dot(
         act_ref[...], down_ref[:, span], preferred_element_type=jnp.float32
     ).astype(jnp.bfloat16)
+    residual = hidden_ref[:, span]
+    send_ref[rows:, :] = jnp.concatenate([residual, residual], axis=0)
 
 
 def third_kernel(act_ref, down_ref, own_ref):
@@ -141,52 +199,90 @@
     own_ref[...] = jnp.dot(act_ref[...], down_ref[:, span], preferred_element_type=jnp.float32)
 
 
-def add_kernel(own_ref, came_ref, out_ref):
-    total = own_ref[...] + came_ref[...].astype(jnp.float32)
-    out_ref[...] = total.astype(jnp.bfloat16).reshape(out_ref.shape)
-
-
-def embed_kernel(parts_ref, hidden_ref, gain_ref, route_ref, out_ref):
-    devices, q_dev, half = parts_ref.shape
-    width = 2 * half
-    totals = [parts_ref[core].astype(jnp.float32) for core in range(2)]
-    for k in range(2, devices):
-        totals[k % 2] += parts_ref[k].astype(jnp.float32)
-    total = jnp.concatenate(totals, axis=1)
-    scaled = gain_ref[...] * (hidden_ref[...].astype(jnp.float32) + total)
-    embedded = scaled * lax.rsqrt(jnp.sum(scaled * scaled, axis=-1, keepdims=True) + 1e-06)
-    query = route_ref[:, 0:1]
-    sent = jnp.zeros((query.shape[0], width), jnp.float32)
-    for q in range(q_dev):
-        sent = jnp.where(query == q, embedded[q : q + 1, :], sent)
-    out_ref[:, :, :width] = sent.astype(jnp.bfloat16).reshape(out_ref.shape[:2] + (width,))
-    lane = lax.broadcasted_iota(jnp.int32, (query.shape[0], LANES), 1)
-    local = jnp.where(lane == 0, route_ref[:, 1:2], 0).astype(jnp.float32)
-    out_ref[:, :, width:] = local.astype(jnp.bfloat16).reshape(out_ref.shape[:2] + (LANES,))
-
-
-def score_kernel(came_ref, codes_ref, scales_ref, out_ref, rows_ref):
-    sources, slots, _ = came_ref.shape
-    lists, list_rows, width = codes_ref.shape
-    pairs = sources * slots
-    came = came_ref[...].reshape(pairs, width + LANES)
+def side_kernel(own_ref, came_ref, hidden_ref, keep_ref, send_ref):
+    rows, half = own_ref.shape
+    q_dev = hidden_ref.shape[0]
+    me = lax.axis_index("wide")
+    core, side, plane = lax.rem(me, 2), lax.rem(me, 4) // 2, me // 4
+    group = 2 * q_dev
+    mine = jnp.where(core == 0, hidden_ref[:, :half], hidden_ref[:, half:]).astype(jnp.float32)
+    other = came_ref[rows : rows + q_dev, :].astype(jnp.float32)
+    residual = jnp.where(
+        core == 0,
+        jnp.concatenate([mine, other], axis=0),
+        jnp.concatenate([other, mine], axis=0),
+    )
+    for z in range(rows // (2 * group)):
+        total = []
+        for y in range(2):
+            span = slice((2 * z + y) * group, (2 * z + y + 1) * group)
+            total.append(own_ref[span, :] + came_ref[span, :].astype(jnp.float32))
+        kept = jnp.where(side == 0, total[0], total[1])
+        sent = jnp.where(side == 0, total[1], total[0])
+        span = slice(z * group, (z + 1) * group)
+        keep_ref[span, :] = kept + jnp.where(plane == z, residual, jnp.zeros_like(residual))
+        send_ref[span, :] = sent.astype(jnp.bfloat16)
+
+
+def sum_kernel(keep_ref, came_ref, after_ref, total_ref, send_ref):
+    total = keep_ref[...] + came_ref[...].astype(jnp.float32)
+    total_ref[...] = total
+    send_ref[...] = total.astype(jnp.bfloat16)
+
+
+def scale_kernel(keep_ref, came_ref, gain_ref, out_ref):
+    rows, half = keep_ref.shape
+    core = lax.rem(lax.axis_index("wide"), 2)
+    gain = jnp.where(core == 0, gain_ref[:, :half], gain_ref[:, half:])
+    scaled = gain * (keep_ref[...] + came_ref[...].astype(jnp.float32))
+    out_ref[:, :half] = scaled.astype(jnp.bfloat16)
+    left = jnp.sum(scaled * scaled, axis=-1, keepdims=True)
+    lane = lax.broadcasted_iota(jnp.int32, (rows, LANES), 1)
+    tail = jnp.zeros((rows, LANES), jnp.float32)
+    for piece in range(3):
+        part = left.astype(jnp.bfloat16).astype(jnp.float32)
+        tail = jnp.where(lane == piece, part, tail)
+        left = left - part
+    out_ref[:, half:] = tail.astype(jnp.bfloat16)
+
+
+def half_scores(mine, near_ref, far_ref, wanted_ref, codes_ref, scales_ref, picks_ref, rows_ref):
+    side_rows, wide = near_ref.shape
+    half = wide - LANES
+    lists, list_rows, _ = codes_ref.shape
+    pairs = wanted_ref.shape[0]
+    core = lax.rem(lax.axis_index("wide"), 2)
+    which = core if mine else 1 - core
+    row = wanted_ref[:, 0:1]
+    local = wanted_ref[:, 1:2]
+    column = lax.broadcasted_iota(jnp.int32, (pairs, side_rows), 1)
+
+    def pick(ref, first):
+        hot = jnp.where(column + first == row, 1.0, 0.0).astype(jnp.bfloat16)
+        return jnp.dot(hot, ref[...], preferred_element_type=jnp.float32)
+
+    chosen = pick(near_ref, 0) + pick(far_ref, side_rows)
+    picks_ref[...] = chosen.astype(jnp.bfloat16)
     nothing = jnp.zeros((pairs, BLOCK), jnp.bfloat16)
-    for block in range(width // BLOCK):
+    for block in range(half // BLOCK):
         span = slice(block * BLOCK, (block + 1) * BLOCK)
         kept = block % 2
-        rows_ref[kept * pairs : (kept + 1) * pairs, span] = came[:, span]
+        rows_ref[kept * pairs : (kept + 1) * pairs, span] = picks_ref[:, span]
         rows_ref[(1 - kept) * pairs : (2 - kept) * pairs, span] = nothing
-    local = came[:, width : width + 1].astype(jnp.float32).astype(jnp.int32)
-
+    squares = jnp.sum(chosen[:, half:], axis=1, keepdims=True)
+
+    blocks = half // BLOCK
     picked = jnp.zeros((pairs, list_rows), jnp.float32)
+    here = pl.ds(pl.multiple_of(which * blocks, blocks), blocks)
     for first in range(0, lists, 2):
-        scale = jnp.concatenate([scales_ref[first], scales_ref[first + 1]], axis=1)
+        scale = jnp.concatenate([scales_ref[first, here, :], scales_ref[first + 1, here, :]], axis=1)
         total = jnp.zeros((pairs, 2 * list_rows), jnp.float32)
-        for step in range(width // (2 * BLOCK)):
+        for step in range(blocks // 2):
             span = slice(step * 2 * BLOCK, (step + 1) * 2 * BLOCK)
+            away = pl.ds(pl.multiple_of(which * half + step * 2 * BLOCK, 2 * BLOCK), 2 * BLOCK)
             part = lax.dot_general(
                 rows_ref[:, span],
-                codes_ref[first : first + 2, :, span].reshape(2 * list_rows, 2 * BLOCK),
+                codes_ref[first : first + 2, :, away].reshape(2 * list_rows, 2 * BLOCK),
                 (((1,), (1,)), ((), ())),
                 preferred_element_type=jnp.float32,
             )
@@ -194,7 +290,31 @@
             total += part[pairs:] * scale[2 * step + 1 : 2 * step + 2, :]
         picked = jnp.where(local == first, total[:, :list_rows], picked)
         picked = jnp.where(local == first + 1, total[:, list_rows:], picked)
-    out_ref[...] = picked.reshape(out_ref.shape)
+    return picked, squares
+
+
+def near_scores_kernel(
+    near_ref, far_ref, wanted_ref, codes_ref, scales_ref, picked_ref, squares_ref, picks_ref, rows_ref
+):
+    picked, squares = half_scores(
+        True, near_ref, far_ref, wanted_ref, codes_ref, scales_ref, picks_ref, rows_ref
+    )
+    picked_ref[...] = picked
+    squares_ref[...] = jnp.broadcast_to(squares, squares_ref.shape)
+
+
+def scores_kernel(
+    near_ref, far_ref, wanted_ref, codes_ref, scales_ref, picked_ref, squares_ref, out_ref,
+    picks_ref, rows_ref,
+):
+    picked, squares = half_scores(
+        False, near_ref, far_ref, wanted_ref, codes_ref, scales_ref, picks_ref, rows_ref
+    )
+    scale = lax.rsqrt(squares_ref[:, 0:1] + squares + 1e-06)
+    scores = (picked_ref[...] + picked) * scale
+    devices, capacity, _ = out_ref.shape
+    for rank in range(capacity):
+        out_ref[:, rank, :] = scores[rank * devices : (rank + 1) * devices]
 
 
 def best_kernel(back_ref, route_ref, out_ref):
@@ -242,12 +362,14 @@
     rows = n * q_dev
     lists_dev, list_rows, _ = codes.shape
     capacity = (q_dev * PROBES + n - 1) // n
-    swap = [(i, i ^ 1) for i in range(n)]
     mib = 1 << 20
     f32, bf16 = jnp.float32, jnp.bfloat16
 
     def exchange(x):
         return lax.all_to_all(x, "wide", 0, 0, tiled=True)
+
+    def swapped(x, bit):
+        return lax.ppermute(x, "wide", [(i, i ^ bit) for i in range(n)])
 
     gate_near = pltpu.with_memory_space_constraint(gate_weight, VMEM)
     up_near = pltpu.with_memory_space_constraint(up_weight, VMEM)
@@ -256,34 +378,30 @@
 
     normed = pl.pallas_call(
         norm_kernel,
-        out_shape=shaped((q_dev, width), bf16),
-        in_specs=[pl.BlockSpec(memory_space=pltpu.HBM)] * 2,
+        out_shape=shaped((q_dev, width + LANES), bf16),
+        in_specs=[pl.BlockSpec(memory_space=pltpu.HBM)] * 3,
         out_specs=pl.BlockSpec(memory_space=VMEM),
         scratch_shapes=[
             VMEM((q_dev, width), bf16),
             VMEM((1, width), f32),
-            pltpu.SemaphoreType.DMA((2,)),
+            VMEM(probes.shape, jnp.int32),
+            pltpu.SemaphoreType.DMA((3,)),
         ],
         compiler_params=pltpu.CompilerParams(vmem_limit_bytes=8 * mib),
     )(
         pltpu.with_memory_space_constraint(hidden_in, pltpu.HBM),
         pltpu.with_memory_space_constraint(ffn_gain[None], pltpu.HBM),
+        pltpu.with_memory_space_constraint(probes, pltpu.HBM),
     )
     spread = call(
         spread_kernel,
-        shaped((n, q_dev, half), bf16),
+        shaped((n, q_dev, half + LANES), bf16),
         (normed,),
         8 * mib,
         cost=ahead(gate_weight, up_weight, down_weight),
     )
     here = exchange(spread)
-    there = lax.ppermute(here, "wide", swap)
-    route = call(
-        functools.partial(route_kernel, lists_dev, capacity),
-        shaped((n * capacity, LANES), jnp.int32),
-        (probes, list_slot[None], counts[None], here),
-        8 * mib,
-    )
+    there = swapped(here, 1)
     gate_part, up_part = call(
         first_kernel,
         [shaped((rows, hidden_units), f32)] * 2,
@@ -294,12 +412,12 @@
     )
     act, sent = call(
         second_kernel,
-        [shaped((rows, hidden_units), bf16), shaped((rows, half), bf16)],
-        (there, gate_part, up_part, gate_near, up_near, down_near, route),
+        [shaped((rows, hidden_units), bf16), shaped((rows + 2 * q_dev, half), bf16)],
+        (there, gate_part, up_part, gate_near, up_near, down_near, hidden_in),
         8 * mib,
         scratch=[VMEM((rows, half), bf16)],
     )
-    came = lax.ppermute(sent, "wide", swap)
+    came = swapped(sent, 1)
     own = call(
         third_kernel,
         shaped((rows, half), f32),
@@ -307,22 +425,65 @@
         8 * mib,
         cost=products(rows * half * hidden_units),
     )
-    pairs_sum = call(add_kernel, shaped((n, q_dev, half), bf16), (own, came), 16 * mib)
-    parts = exchange(pairs_sum)
-    queries = call(
-        embed_kernel,
-        shaped((n, capacity, width + LANES), bf16),
-        (parts, hidden_in, final_gain[None], route),
-        16 * mib,
-        cost=ahead(codes),
-    )
-    recv = exchange(queries)
+    side_rows = rows // 2
+    keep, sent = call(
+        side_kernel,
+        [shaped((side_rows, half), f32), shaped((side_rows, half), bf16)],
+        (own, came, hidden_in),
+        8 * mib,
+    )
+    route = call(
+        functools.partial(route_kernel, lists_dev, capacity),
+        shaped((n * capacity, LANES), jnp.int32),
+        (probes, list_slot[None], counts[None], keep),
+        4 * mib,
+    )
+    wanted = call(
+        functools.partial(wanted_kernel, capacity, q_dev, PROBES),
+        shaped((n * capacity, LANES), jnp.int32),
+        (here, list_slot[None], route),
+        4 * mib,
+    )
+    came = swapped(sent, 2)
+    bit = 4
+    while bit < n:
+        keep, sent = call(
+            sum_kernel,
+            [shaped((side_rows, half), f32), shaped((side_rows, half), bf16)],
+            (keep, came, wanted),
+            8 * mib,
+            cost=ahead(codes) if bit == 4 else None,
+        )
+        came = swapped(sent, bit)
+        bit *= 2
+    near = call(
+        scale_kernel,
+        shaped((side_rows, half + LANES), bf16),
+        (keep, came, final_gain[None]),
+        8 * mib,
+    )
+    far = swapped(near, 2)
+    near_other = swapped(near, 1)
+    far_other = swapped(far, 1)
+    scales_near = jnp.swapaxes(scales, 1, 2)
+    scratch = [
+        VMEM((n * capacity, half + LANES), bf16),
+        VMEM((2 * n * capacity, half), bf16),
+    ]
+    picked, squares = call(
+        near_scores_kernel,
+        [shaped((n * capacity, list_rows), f32), shaped((n * capacity, LANES), f32)],
+        (near, far, wanted, codes_near, scales_near),
+        8 * mib,
+        cost=products(n * capacity * lists_dev * list_rows * width),
+        scratch=scratch,
+    )
     scores = call(
-        score_kernel,
+        scores_kernel,
         shaped((n, capacity, list_rows), f32),
-        (recv, codes_near, jnp.swapaxes(scales, 1, 2)),
-        20 * mib,
-        scratch=[VMEM((2 * n * capacity, width), bf16)],
+        (near_other, far_other, wanted, codes_near, scales_near, picked, squares),
+        8 * mib,
+        scratch=scratch,
     )
     back = exchange(scores)
     return call(best_kernel, shaped((q_dev, K_TOP), f32), (back, route), 8 * mib)

time: 64.2 us -> 61.8 us (0.963)
  blocking collectives: 52.6 us -> 27.2 us
  waiting for transfers between devices: 0.4 us -> 20.2 us
  starting transfers between devices: 0.56 us -> 3.22 us
  Pallas kernels: 9.97 us -> 10.7 us
    all_to_all x4 -> x2, blocking collectives: 52.6 us -> 27.2 us  [exchange(): return lax.all_to_all(x, 'wide', 0, 0, tiled=True)]
    ppermute x2 -> x8, waiting for transfers between devices: 0.4 us -> 20.2 us  [swapped(): return lax.ppermute(x, 'wide', [(i, i ^ bit) for i in range(n)])]
    ppermute x2 -> x8, starting transfers between devices: 0.56 us -> 3.22 us  [swapped(): return lax.ppermute(x, 'wide', [(i, i ^ bit) for i in range(n)])]
    pallas_call x9 -> x13, Pallas kernels: 9.06 us -> 9.82 us  [call(): pl.pallas_call(kernel, out_shape=out_shape, in_specs=[pl.BlockSpec(memory...]
  transfers between devices with their start and end apart: 2 -> 8, of which waited for: 1 -> 6; matrix products, arithmetic and copies ran while one was open for 0% -> 0% of each run, Pallas kernels for 4% -> 7%
where the time goes in v4:
time: 61.8 us; the launch traced here: 61.6 us
  blocking collectives  27.2 us (44%)
  waiting for transfers between devices  20.2 us (33%)
  Pallas kernels  10.7 us (17%)
  starting transfers between devices  3.22 us (5%)
    all_to_all x2, blocking collectives, exchange(): return lax.all_to_all(x, 'wide', 0, 0, tiled=True)  27.2 us
    ppermute x8, waiting for transfers between devices, swapped(): return lax.ppermute(x, 'wide', [(i, i ^ bit) for i in range(n)])  20.2 us
    pallas_call x13, Pallas kernels, call(): pl.pallas_call(kernel, out_shape=out_shape, in_specs=[pl.BlockSpec(memory...  9.82 us
    ppermute x8, starting transfers between devices, swapped(): return lax.ppermute(x, 'wide', [(i, i ^ bit) for i in range(n)])  3.22 us
  transfers between devices with their start and end apart: 8, of which 6 were waited for; matrix products, arithmetic and copies ran while one was open for 0% of the time, Pallas kernels for 7%

profile of v4, /device:TPU:0, one launch (start us, length us, event | category | flops | bytes accessed | tf_op | source)
XLA Modules:
  0.0 61.6 jit_solution(11891561836023870944)
XLA Ops:
  0.0 0.9 %shard_map.109.normed_ref = bf16[4,4224]{1,0:T(4,128)(2,1)S(1)} custom-call(bf16[4,4096]{1,0:T(4,128)(2,1)} %hidden_ref.5, f32[1,4096]{1,0:T(1,128)} %bitcast.13, s32[4,8]{1,0:T(4,128)} %probes_ref.3), custom_call_target="tpu_custom_call" | custom-call | tf_op jit(solution)/shard_map/pallas_call | solution.py:379
  1.0 17.8 %all_to_all.10.here_ref = bf16[16,4,2176]{2,1,0:T(4,128)(2,1)S(1)} all-to-all(bf16[16,4,2176]{2,1,0:T(4,128)(2,1)S(1)} %shard_map.110), channel_id=1, replica_groups=mesh['grp'=2,'wide'=16] {'wide'}, dimensions={0} | all-to-all | bytes 557056 | tf_op jit(solution)/shard_map/all_to_all | solution.py:369
  18.8 0.1 collective-permute-start
  18.9 1.4 %shard_map.111 = (f32[64,896]{1,0:T(8,128)S(1)}, f32[64,896]{1,0:T(8,128)S(1)}) custom-call(bf16[16,4,2176]{2,1,0:T(4,128)(2,1)S(1)} %all_to_all.10.here_ref, bf16[4096,896]{1,0:T(8,128)(2,1)S(1)} %copy-done.1, bf16[4096,896]{1,0:T(8,128)(2,1)S(1)} %copy-done.2, bf16[896,4096]{1,0:T(8,128)(2,1)S(1)} %copy-done), custom_call_target="tpu_custom_call" | custom-call | flops 469762048 | bytes 1048576 | tf_op jit(solution)/shard_map/pallas_call | solution.py:23
  20.3 2.0 %shard_map.112 = (bf16[64,896]{1,0:T(8,128)(2,1)S(1)}, bf16[72,2048]{1,0:T(8,128)(2,1)S(1)}) custom-call(bf16[16,4,2176]{2,1,0:T(4,128)(2,1)S(1)} %collective-permute-done.there_ref, f32[64,896]{1,0:T(8,128)S(1)} %get-tuple-element.17.gate_part, f32[64,896]{1,0:T(8,128)S(1)} %get-tuple-element.18.up_part, bf16[4096,896]{1,0:T(8,128)(2,1)S(1)} %copy-done.1, ...), custom_call_target="tpu_custom_call" | custom-call | tf_op jit(solution)/shard_map/pallas_call | solution.py:23
  22.4 0.4 collective-permute-start.1
  22.8 0.8 %shard_map.113.own_ref = f32[64,2048]{1,0:T(8,128)S(1)} custom-call(bf16[64,896]{1,0:T(8,128)(2,1)S(1)} %get-tuple-element.19.act_ref, bf16[896,4096]{1,0:T(8,128)(2,1)S(1)} %copy-done), custom_call_target="tpu_custom_call" | custom-call | flops 234881024 | bytes 1048576 | tf_op jit(solution)/shard_map/pallas_call | solution.py:23
  23.6 0.5 collective-permute-done.1.came_ref
  24.0 0.1 shard_map.114
  24.1 0.5 collective-permute-start.2
  24.6 0.3 shard_map.115.after_ref.route_ref
  25.0 0.5 shard_map.116.after_ref.wanted_ref
  25.5 4.4 %collective-permute-done.2.came_ref = bf16[32,2048]{1,0:T(8,128)(2,1)S(1)} collective-permute-done((bf16[32,2048]{1,0:T(8,128)(2,1)S(1)}, bf16[32,2048]{1,0:T(8,128)(2,1)S(1)}, u32[]{:S(2)}, u32[]{:S(2)}) %collective-permute-start.2) | collective-permute-done | bytes 131104 | tf_op jit(solution)/shard_map/ppermute | solution.py:372
  30.0 0.5 collective-permute-start.3
  30.5 4.5 %collective-permute-done.3.came_ref = bf16[32,2048]{1,0:T(8,128)(2,1)S(1)} collective-permute-done((bf16[32,2048]{1,0:T(8,128)(2,1)S(1)}, bf16[32,2048]{1,0:T(8,128)(2,1)S(1)}, u32[]{:S(2)}, u32[]{:S(2)}) %collective-permute-start.3) | collective-permute-done | bytes 131104 | tf_op jit(solution)/shard_map/ppermute | solution.py:372
  35.1 1.2 %collective-permute-start.4 = (bf16[32,2048]{1,0:T(8,128)(2,1)S(1)}, bf16[32,2048]{1,0:T(8,128)(2,1)S(1)}, u32[]{:S(2)}, u32[]{:S(2)}) collective-permute-start(bf16[32,2048]{1,0:T(8,128)(2,1)S(1)} %get-tuple-element.26), channel_id=1, source_target_pairs={{0,8},{1,9},{2,10},{3,11},{4,12},{5,13},{6,14},{7,15},{8,0},{9,1},... | collective-permute-start | bytes 393224 | tf_op jit(solution)/shard_map/ppermute | solution.py:372
  36.3 6.0 %collective-permute-done.4.came_ref = bf16[32,2048]{1,0:T(8,128)(2,1)S(1)} collective-permute-done((bf16[32,2048]{1,0:T(8,128)(2,1)S(1)}, bf16[32,2048]{1,0:T(8,128)(2,1)S(1)}, u32[]{:S(2)}, u32[]{:S(2)}) %collective-permute-start.4) | collective-permute-done | bytes 131104 | tf_op jit(solution)/shard_map/ppermute | solution.py:372
  42.3 0.1 shard_map.119.near_ref
  42.4 0.5 collective-permute-start.6
  42.9 4.6 %collective-permute-done.6.far_ref = bf16[32,2176]{1,0:T(8,128)(2,1)S(1)} collective-permute-done((bf16[32,2176]{1,0:T(8,128)(2,1)S(1)}, bf16[32,2176]{1,0:T(8,128)(2,1)S(1)}, u32[]{:S(2)}, u32[]{:S(2)}) %collective-permute-start.6) | collective-permute-done | bytes 139296 | tf_op jit(solution)/shard_map/ppermute | solution.py:372
  47.6 1.5 %shard_map.120 = (f32[32,128]{1,0:T(8,128)S(1)}, f32[32,128]{1,0:T(8,128)S(1)}) custom-call(bf16[32,2176]{1,0:T(8,128)(2,1)S(1)} %shard_map.119.near_ref, bf16[32,2176]{1,0:T(8,128)(2,1)S(1)} %collective-permute-done.6.far_ref, s32[32,128]{1,0:T(8,128)S(1)} %shard_map.116.after_ref.wanted_ref, bf16[8,128,4096]{2,1,0:T(8,128)(2,1)S(1)} %bitcast.6, ...), custom_call_target="tpu_custom_call" | custom-call | flops 268435456 | bytes 1048576 | tf_op jit(solution)/shard_map/pallas_call | solution.py:23
  49.2 1.6 %shard_map.121 = f32[16,2,128]{2,1,0:T(2,128)S(1)} custom-call(bf16[32,2176]{1,0:T(8,128)(2,1)S(1)} %collective-permute-done.5.near_ref, bf16[32,2176]{1,0:T(8,128)(2,1)S(1)} %collective-permute-done.7.far_ref, s32[32,128]{1,0:T(8,128)S(1)} %shard_map.116.after_ref.wanted_ref, bf16[8,128,4096]{2,1,0:T(8,128)(2,1)S(1)} %bitcast.6, f32[8,32,128]{2,1,0:T(8,128)S(1)} %bitcast.8, ...), custom_call_target="tpu_custom_call" | custom-call | tf_op jit(solution)/shard_map/pallas_call | solution.py:23
  50.7 9.5 %all_to_all.11.back_ref = f32[16,2,128]{2,1,0:T(2,128)S(1)} all-to-all(f32[16,2,128]{2,1,0:T(2,128)S(1)} %shard_map.121), channel_id=1, replica_groups=mesh['grp'=2,'wide'=16] {'wide'}, dimensions={0} | all-to-all | bytes 32768 | tf_op jit(solution)/shard_map/all_to_all | solution.py:369
  60.2 1.4 %shard_map.122 = f32[4,8]{1,0:T(4,128)} custom-call(f32[16,2,128]{2,1,0:T(2,128)S(1)} %all_to_all.11.back_ref, s32[32,128]{1,0:T(8,128)S(1)} %shard_map.115.after_ref.route_ref), custom_call_target="tpu_custom_call" | custom-call | tf_op jit(solution)/shard_map/pallas_call | solution.py:23
  (31 shorter events, 0.2 us)
Async XLA Ops:
  0.9 17.9 %copy-start = (bf16[896,4096]{1,0:T(8,128)(2,1)S(1)}, bf16[896,4096]{1,0:T(8,128)(2,1)}, u32[]{:S(2)}) copy-start(bf16[896,4096]{1,0:T(8,128)(2,1)} %down_ref.3) | copy-start | bytes 22020100
  0.9 17.9 %copy-start.1 = (bf16[4096,896]{1,0:T(8,128)(2,1)S(1)}, bf16[4096,896]{1,0:T(8,128)(2,1)}, u32[]{:S(2)}) copy-start(bf16[4096,896]{1,0:T(8,128)(2,1)} %gate_ref.3) | copy-start | bytes 22020100
  1.0 17.9 %copy-start.2 = (bf16[4096,896]{1,0:T(8,128)(2,1)S(1)}, bf16[4096,896]{1,0:T(8,128)(2,1)}, u32[]{:S(2)}) copy-start(bf16[4096,896]{1,0:T(8,128)(2,1)} %up_ref.3) | copy-start | bytes 22020100
  18.8 1.6 %copy-start.4 = (bf16[4,4096]{1,0:T(4,128)(2,1)S(1)}, bf16[4,4096]{1,0:T(4,128)(2,1)}, u32[]{:S(2)}) copy-start(bf16[4,4096]{1,0:T(4,128)(2,1)} %hidden_ref.5) | copy-start | bytes 98308
  18.8 1.6 %collective-permute-start = (bf16[16,4,2176]{2,1,0:T(4,128)(2,1)S(1)}, bf16[16,4,2176]{2,1,0:T(4,128)(2,1)S(1)}, u32[]{:S(2)}, u32[]{:S(2)}) collective-permute-start(bf16[16,4,2176]{2,1,0:T(4,128)(2,1)S(1)} %all_to_all.10.here_ref), channel_id=1, source_target_pairs={{0,1},{1,0},{2,3},{3,2},{4,5},{5,4},{6,7},{7,6},{8,9},{9,8},{10,11... | collective-permute-start | bytes 835592 | tf_op jit(solution)/shard_map/ppermute | solution.py:372
  22.3 2.3 %copy-start.6 = (s32[4,8]{1,0:T(4,128)S(1)}, s32[4,8]{1,0:T(4,128)}, u32[]{:S(2)}) copy-start(s32[4,8]{1,0:T(4,128)} %probes_ref.3) | copy-start | bytes 388
  22.4 2.3 %copy-start.7 = (s32[128]{0:T(128)S(1)}, s32[128]{0:T(128)}, u32[]{:S(2)}) copy-start(s32[128]{0:T(128)} %param.20) | copy-start | bytes 1540
  22.4 2.3 %copy-start.8 = (s32[128]{0:T(128)S(1)}, s32[128]{0:T(128)}, u32[]{:S(2)}) copy-start(s32[128]{0:T(128)} %param.19) | copy-start | bytes 1540
  22.4 1.6 %collective-permute-start.1 = (bf16[72,2048]{1,0:T(8,128)(2,1)S(1)}, bf16[72,2048]{1,0:T(8,128)(2,1)S(1)}, u32[]{:S(2)}, u32[]{:S(2)}) collective-permute-start(bf16[72,2048]{1,0:T(8,128)(2,1)S(1)} %get-tuple-element.20), channel_id=1, source_target_pairs={{0,1},{1,0},{2,3},{3,2},{4,5},{5,4},{6,7},{7,6},{8,9},{9,8},{10,11... | collective-permute-start | bytes 884744 | tf_op jit(solution)/shard_map/ppermute | solution.py:372
  24.1 5.8 %collective-permute-start.2 = (bf16[32,2048]{1,0:T(8,128)(2,1)S(1)}, bf16[32,2048]{1,0:T(8,128)(2,1)S(1)}, u32[]{:S(2)}, u32[]{:S(2)}) collective-permute-start(bf16[32,2048]{1,0:T(8,128)(2,1)S(1)} %get-tuple-element.22), channel_id=1, source_target_pairs={{0,2},{1,3},{2,0},{3,1},{4,6},{5,7},{6,4},{7,5},{8,10},{9,11},{10,... | collective-permute-start | bytes 393224 | tf_op jit(solution)/shard_map/ppermute | solution.py:372
  25.0 22.6 %slice-start = ((s8[8388608]{0:T(1024)(128)(4,1)}), s8[4194304]{0:T(1024)(128)(4,1)S(1)}, s32[]{:S(2)}) async-start(s8[8388608]{0:T(1024)(128)(4,1)} %bitcast.5), calls=%async_computation.2 | async-start | bytes 8388608
  25.5 16.8 %copy-start.5 = (f32[4096]{0:T(1024)S(1)}, f32[4096]{0:T(1024)}, u32[]{:S(2)}) copy-start(f32[4096]{0:T(1024)} %param.16) | copy-start | bytes 49156
  25.5 22.1 %slice-start.1 = ((s8[8388608]{0:T(1024)(128)(4,1)}), s8[4194304]{0:T(1024)(128)(4,1)S(1)}, s32[]{:S(2)}) async-start(s8[8388608]{0:T(1024)(128)(4,1)} %bitcast.5), calls=%async_computation.3 | async-start | bytes 8388608
  25.5 22.1 %copy-start.3 = (f32[8,128,32]{1,2,0:T(8,128)S(1)}, f32[8,128,32]{1,2,0:T(8,128)}, u32[]{:S(2)}) copy-start(f32[8,128,32]{1,2,0:T(8,128)} %param.18) | copy-start | bytes 393220
  30.0 5.0 %collective-permute-start.3 = (bf16[32,2048]{1,0:T(8,128)(2,1)S(1)}, bf16[32,2048]{1,0:T(8,128)(2,1)S(1)}, u32[]{:S(2)}, u32[]{:S(2)}) collective-permute-start(bf16[32,2048]{1,0:T(8,128)(2,1)S(1)} %get-tuple-element.24), channel_id=1, source_target_pairs={{0,4},{1,5},{2,6},{3,7},{4,0},{5,1},{6,2},{7,3},{8,12},{9,13},{10,... | collective-permute-start | bytes 393224 | tf_op jit(solution)/shard_map/ppermute | solution.py:372
  35.1 7.2 %collective-permute-start.4 = (bf16[32,2048]{1,0:T(8,128)(2,1)S(1)}, bf16[32,2048]{1,0:T(8,128)(2,1)S(1)}, u32[]{:S(2)}, u32[]{:S(2)}) collective-permute-start(bf16[32,2048]{1,0:T(8,128)(2,1)S(1)} %get-tuple-element.26), channel_id=1, source_target_pairs={{0,8},{1,9},{2,10},{3,11},{4,12},{5,13},{6,14},{7,15},{8,0},{9,1},... | collective-permute-start | bytes 393224 | tf_op jit(solution)/shard_map/ppermute | solution.py:372
  42.4 5.1 %collective-permute-start.6 = (bf16[32,2176]{1,0:T(8,128)(2,1)S(1)}, bf16[32,2176]{1,0:T(8,128)(2,1)S(1)}, u32[]{:S(2)}, u32[]{:S(2)}) collective-permute-start(bf16[32,2176]{1,0:T(8,128)(2,1)S(1)} %shard_map.119.near_ref), channel_id=1, source_target_pairs={{0,2},{1,3},{2,0},{3,1},{4,6},{5,7},{6,4},{7,5},{8,10},{9,11},{10,... | collective-permute-start | bytes 417800 | tf_op jit(solution)/shard_map/ppermute | solution.py:372
  42.9 6.2 %collective-permute-start.5 = (bf16[32,2176]{1,0:T(8,128)(2,1)S(1)}, bf16[32,2176]{1,0:T(8,128)(2,1)S(1)}, u32[]{:S(2)}, u32[]{:S(2)}) collective-permute-start(bf16[32,2176]{1,0:T(8,128)(2,1)S(1)} %shard_map.119.near_ref), channel_id=1, source_target_pairs={{0,1},{1,0},{2,3},{3,2},{4,5},{5,4},{6,7},{7,6},{8,9},{9,8},{10,11... | collective-permute-start | bytes 417800 | tf_op jit(solution)/shard_map/ppermute | solution.py:372
  47.6 1.6 %collective-permute-start.7 = (bf16[32,2176]{1,0:T(8,128)(2,1)S(1)}, bf16[32,2176]{1,0:T(8,128)(2,1)S(1)}, u32[]{:S(2)}, u32[]{:S(2)}) collective-permute-start(bf16[32,2176]{1,0:T(8,128)(2,1)S(1)} %collective-permute-done.6.far_ref), channel_id=1, source_target_pairs={{0,1},{1,0},{2,3},{3,2},{4,5},{5,4},{6,7},{7,6},{8,9},{9,8},{10,11... | collective-permute-start | bytes 417800 | tf_op jit(solution)/shard_map/ppermute | solution.py:372
